TPU v7x, 512 devices: a whole 4x4x16 slice. The times are simulated.
512 devices in a mesh: quad: 16 (over y, x), tile: 32 (over z, core).
Axes of the slice: x: 4, y: 4, z: 16, core: 2. Of those that a mesh axis runs over, the one named last changes fastest.
Arguments:
- blocks: bfloat16 [2048, 6, 256, 256], P(('quad', 'tile')), may hold values from -4 to 4
- offsets: int32 [2048, 6], P(('quad', 'tile')), may hold values from -3 to 3, as said below
- sketch: bfloat16 [524288, 512], P(('quad', 'tile')), may hold values from -6 to 6
- leaf_pivots: int32 [2048, 128], P(('quad', 'tile')), may hold values from 0 to 255, as said below
- node_pivots: int32 [512, 128], P(('quad', 'tile')), may hold values from 0 to 511, as said below
- pair_pivots: int32 [512, 64], P(('quad', 'tile')), may hold values from 0 to 127, as said below
- group_pivots: int32 [512, 32], P(('quad', 'tile')), may hold values from 0 to 63, as said below
Outputs:
- leaf_interp: float32 [524288, 128], P(('quad', 'tile'))
- node_interp: float32 [262144, 128], P(('quad', 'tile'))
- pair_interp: float32 [65536, 128], P(('quad', 'tile'))
- group_interp: float32 [32768, 128], P(('quad', 'tile'))
Inputs may be any that keep to these rules, and one draw needn't show every extreme that they name: `offsets`: each row holds distinct values in rising order. `leaf_pivots`: each row holds distinct values in rising order. `node_pivots`: each row holds distinct values in rising order. `pair_pivots`: each row holds distinct values in rising order. `group_pivots`: each row holds distinct values in rising order.
All inputs are finite; a program needn't handle non-finite values.
Results may differ from a plain program's by a relative error of at most 0.0003.
Values may be sent and summed in bfloat16 or wider, within the bound.
A program may use at most 64 MiB of HBM per device.

v0:
```python
import jax
import jax.numpy as jnp
from jax import lax
from jax.sharding import PartitionSpec as P

HALF = 3


def padded_2(block, sides, width):
    for axis, dim in sides:
        count = lax.axis_size(axis)
        forward = [(i, i + 1) for i in range(count - 1)]
        backward = [(target, source) for source, target in forward]
        low = lax.ppermute(
            lax.slice_in_dim(block, block.shape[dim] - width, None, axis=dim), axis, forward
        )
        high = lax.ppermute(lax.slice_in_dim(block, 0, width, axis=dim), axis, backward)
        block = jnp.concatenate([low, block, high], axis=dim)
    return block


def from_partner(block, axis, bit):
    count = lax.axis_size(axis)
    route = []
    for low in range(count):
        high = low | 1 << bit
        if high != low and high < count:
            route += [(low, high), (high, low)]
    return lax.ppermute(block, axis, route)


def project(rows, skeleton):
    highest = lax.Precision.HIGHEST
    moment = jnp.dot(skeleton, skeleton.T, precision=highest)
    damping = jnp.sum(skeleton * skeleton) / skeleton.shape[0] + 1e-06
    matrix = moment + damping * jnp.eye(skeleton.shape[0], dtype=jnp.float32)
    coupling = jnp.dot(rows, skeleton.T, precision=highest)
    factor = jnp.linalg.cholesky(matrix)
    inner = lax.linalg.triangular_solve(factor, coupling.T, left_side=True, lower=True)
    outer = lax.linalg.triangular_solve(factor, inner, left_side=True, lower=True, transpose_a=True)
    return outer.T


def select_rows(rows, index):
    return jnp.take(rows, index, axis=0)


def ordered(first_low, mine, theirs):
    return jnp.where(
        first_low, jnp.concatenate([mine, theirs], axis=0), jnp.concatenate([theirs, mine], axis=0)
    )


def body(blocks, offsets, sketch, leaf_pivots, node_pivots, pair_pivots, group_pivots):
    leaves = blocks.shape[0]
    width = blocks.shape[2]
    columns = sketch.shape[1]
    padded = padded_2(sketch, ((("quad", "tile"), 0),), HALF * width)
    panels = padded.reshape(leaves + 2 * HALF, width, columns)
    source = jnp.arange(leaves, dtype=jnp.int32)[:, None] + HALF + offsets
    gathered = panels[source]
    sample = jnp.einsum("pkab,pkbr->par", blocks, gathered, preferred_element_type=jnp.float32)
    skeleton = jax.vmap(select_rows)(sample, leaf_pivots)
    leaf_interp = jax.vmap(project)(sample, skeleton)
    stacked = skeleton.reshape(-1, columns)
    node_skel = select_rows(stacked, node_pivots[0])
    node_interp = project(stacked, node_skel)
    upper = select_rows(node_skel, pair_pivots[0])
    higher = select_rows(upper, group_pivots[0])
    position = lax.axis_index("tile")
    lower_half = position % 2 == 0
    sibling_upper, sibling_higher = from_partner((upper, higher), "tile", 0)
    pair_higher = ordered(lower_half, higher, sibling_higher)
    cousin_higher = from_partner(pair_higher, "tile", 1)
    lower_pair = position // 2 % 2 == 0
    group_skel = ordered(lower_pair, pair_higher, cousin_higher)
    pair_skel = ordered(lower_half, upper, sibling_upper)
    pair_interp = project(node_skel, pair_skel)
    group_interp = project(upper, group_skel)
    return (leaf_interp.reshape(leaves * width, -1), node_interp, pair_interp, group_interp)


def solution(mesh):
    placed = (
        P(("quad", "tile"), None, None, None),
        P(("quad", "tile"), None),
        P(("quad", "tile"), None),
        P(("quad", "tile"), None),
        P(("quad", "tile"), None),
        P(("quad", "tile"), None),
        P(("quad", "tile"), None),
    )
    return jax.shard_map(
        body,
        mesh=mesh,
        in_specs=placed,
        out_specs=(
            P(("quad", "tile"), None),
            P(("quad", "tile"), None),
            P(("quad", "tile"), None),
            P(("quad", "tile"), None),
        ),
        check_vma=False,
    )
```

profile of v0, /device:TPU:24, one launch (start us, length us, event | category | flops | bytes accessed | tf_op | source)
XLA Modules:
  0.0 300.6 jit_solution(6289747828285251453)
XLA Ops:
  0.7 2.8 fusion.47
  3.5 13.2 %collective-permute-start.1 = (bf16[768,512]{1,0:T(8,128)(2,1)}, bf16[768,512]{1,0:T(8,128)(2,1)}, u32[]{:S(2)}, u32[]{:S(2)}) collective-permute-start(bf16[768,512]{1,0:T(8,128)(2,1)} %get-tuple-element.8), channel_id=1, source_target_pairs={{1,0},{2,1},{3,2},{4,3},{5,4},{6,5},{7,6},{8,7},{9,8},{10,9},{11,1... | collective-permute-start | bytes 2359304 | tf_op jit(solution)/shard_map/ppermute | solution.py:17
  23.4 3.1 %collective-permute-done.1 = bf16[768,512]{1,0:T(8,128)(2,1)} collective-permute-done((bf16[768,512]{1,0:T(8,128)(2,1)}, bf16[768,512]{1,0:T(8,128)(2,1)}, u32[]{:S(2)}, u32[]{:S(2)}) %collective-permute-start.1) | collective-permute-done | bytes 786464 | tf_op jit(solution)/shard_map/ppermute | solution.py:17
  26.5 8.0 %collective-permute-done = bf16[768,512]{1,0:T(8,128)(2,1)} collective-permute-done((bf16[768,512]{1,0:T(8,128)(2,1)}, bf16[768,512]{1,0:T(8,128)(2,1)}, u32[]{:S(2)}, u32[]{:S(2)}) %collective-permute-start) | collective-permute-done | bytes 786464 | tf_op jit(solution)/shard_map/ppermute | solution.py:14
  34.5 3.4 %pad_maximum_fusion = bf16[2560,512]{1,0:T(8,128)(2,1)} fusion(bf16[768,512]{1,0:T(8,128)(2,1)} %collective-permute-done.1, bf16[1024,512]{1,0:T(8,128)(2,1)} %param.10, bf16[768,512]{1,0:T(8,128)(2,1)} %collective-permute-done), kind=kLoop, calls=%fused_computation.5 | loop fusion | flops 7864320 | bytes 5242880 | tf_op jit(solution)/shard_map/concatenate | solution.py:18
  37.9 6.1 %gather_fusion = bf16[24,256,512]{2,1,0:T(8,128)(2,1)} fusion(bf16[10,256,512]{2,1,0:T(8,128)(2,1)} %bitcast.99, s32[1024]{0:T(1024)S(1)} %pad_clamp_fusion.3), kind=kCustom, calls=%fused_computation | custom fusion | bytes 12583008 | tf_op jit(solution)/shard_map/gather | solution.py:61
  44.1 6.4 %fusion.48 = f32[4,512,256,1]{2,1,3,0:T(8,128)} fusion(bf16[4,6,256,512]{3,2,1,0:T(8,128)(2,1)} %bitcast.103, bf16[4,6,256,256]{3,2,1,0:T(8,128)(2,1)S(1)} %copy-done), kind=kOutput, calls=%fused_computation.106 | convolution fusion | flops 1610612736 | bytes 11534336 | tf_op jit(solution)/shard_map/pkab,pkbr->par/dot_general | solution.py:62
  50.4 2.9 copy.22
  53.4 9.3 %gather_fusion.4 = f32[512,512]{1,0:T(8,128)} fusion(f32[4,256,512]{2,1,0:T(8,128)} %copy.22, s32[512]{0:T(512)S(1)} %fusion.37), kind=kCustom, calls=%fused_computation.4 | custom fusion | bytes 2101248 | tf_op jit(solution)/shard_map/vmap(jit(_take))/gather | solution.py:45
  62.7 4.2 %fusion = f32[4,128,256]{2,1,0:T(8,128)} fusion(f32[4,512,256,1]{2,1,3,0:T(8,128)} %fusion.48, f32[4,128,512]{2,1,0:T(8,128)} %bitcast.100, pred[4,128]{1,0:T(4,128)(4,1)S(1)} %compare_and_fusion.3), kind=kOutput, calls=%fused_computation.6 | convolution fusion | flops 805568512 | bytes 3670528 | tf_op jit(solution)/shard_map/vmap()/dot_general | solution.py:37
  73.8 47.7 %custom-call.26 = f32[4,128,128]{2,1,0:T(8,128)S(1)} custom-call(f32[4,128,128]{2,1,0:T(8,128)} %fusion.14), custom_call_target="Cholesky" | custom-call | tf_op jit(solution)/shard_map/vmap(jit(cholesky))/cholesky | solution.py:38
  123.2 40.4 %custom-call.27 = f32[4,1,128,128]{2,3,1,0:T(8,128)S(1)} custom-call(f32[4,1,128,128]{3,2,1,0:T(8,128)} %select_bitcast_fusion), custom_call_target="InvertDiagBlocksLowerTriangular" | custom-call | tf_op jit(solution)/shard_map/vmap()/triangular_solve | solution.py:40
  163.5 2.2 fusion.11
  168.3 2.9 gather_fusion.1
  172.9 3.1 %fusion.49 = f32[128,512]{1,0:T(8,128)} fusion(f32[128,512]{1,0:T(8,128)S(1)} %get-tuple-element.6, f32[512,512]{1,0:T(8,128)} %broadcast_select_fusion), kind=kOutput, calls=%fused_computation.107 | convolution fusion | flops 402653184 | bytes 1572864 | tf_op jit(solution)/shard_map/dot_general | solution.py:37
  179.3 12.5 %cholesky.106 = f32[128,128]{1,0:T(8,128)S(1)} custom-call(f32[128,128]{1,0:T(8,128)} %copy.26), custom_call_target="Cholesky" | custom-call | tf_op jit(solution)/shard_map/jit(cholesky)/cholesky | solution.py:38
  193.2 10.4 %custom-call.28 = f32[1,128,128]{1,2,0:T(8,128)} custom-call(f32[1,128,128]{2,1,0:T(8,128)S(1)} %fusion.15), custom_call_target="InvertDiagBlocksLowerTriangular" | custom-call | tf_op jit(solution)/shard_map/triangular_solve | solution.py:40
  210.3 2.4 collective-permute-start.3
  216.9 12.2 %collective-permute-start.4 = (f32[64,512]{1,0:T(8,128)}, f32[64,512]{1,0:T(8,128)}, u32[]{:S(2)}, u32[]{:S(2)}) collective-permute-start(f32[64,512]{1,0:T(8,128)} %maximum_select_fusion.2), channel_id=1, source_target_pairs={{0,2},{2,0},{1,3},{3,1},{4,6},{6,4},{5,7},{7,5},{8,10},{10,8},{9,1... | collective-permute-start | bytes 393224 | tf_op jit(solution)/shard_map/ppermute | solution.py:29
  231.4 2.1 convolution_add_fusion.1
  238.2 13.2 %cholesky.117 = f32[128,128]{1,0:T(8,128)} custom-call(f32[128,128]{1,0:T(8,128)} %copy.28), custom_call_target="Cholesky" | custom-call | tf_op jit(solution)/shard_map/jit(cholesky)/cholesky | solution.py:38
  255.0 11.3 %custom-call.29 = f32[1,128,128]{1,2,0:T(8,128)} custom-call(f32[1,128,128]{2,1,0:T(8,128)} %fusion.16), custom_call_target="InvertDiagBlocksLowerTriangular" | custom-call | tf_op jit(solution)/shard_map/triangular_solve | solution.py:40
  274.9 11.7 %cholesky.128 = f32[128,128]{1,0:T(8,128)S(1)} custom-call(f32[128,128]{1,0:T(8,128)S(1)} %copy.30), custom_call_target="Cholesky" | custom-call | tf_op jit(solution)/shard_map/jit(cholesky)/cholesky | solution.py:38
  287.9 9.8 %custom-call.30 = f32[1,128,128]{1,2,0:T(8,128)S(1)} custom-call(f32[1,128,128]{2,1,0:T(8,128)S(1)} %fusion.17), custom_call_target="InvertDiagBlocksLowerTriangular" | custom-call | tf_op jit(solution)/shard_map/triangular_solve | solution.py:40
  (96 shorter events, 56.1 us)
Async XLA Ops:
  0.6 43.4 %copy-start = (bf16[4,6,256,256]{3,2,1,0:T(8,128)(2,1)S(1)}, bf16[4,6,256,256]{3,2,1,0:T(8,128)(2,1)}, u32[]{:S(2)}) copy-start(bf16[4,6,256,256]{3,2,1,0:T(8,128)(2,1)} %param.8) | copy-start | bytes 9437188
  0.6 18.6 %copy-start.10 = (s32[1,128]{1,0:T(1,128)S(1)}, s32[1,128]{1,0:T(1,128)}, u32[]{:S(2)}) copy-start(s32[1,128]{1,0:T(1,128)} %param.12) | copy-start | bytes 1540
  0.7 19.2 %copy-start.11 = (s32[1,64]{1,0:T(1,128)S(1)}, s32[1,64]{1,0:T(1,128)}, u32[]{:S(2)}) copy-start(s32[1,64]{1,0:T(1,128)} %param.13) | copy-start | bytes 772
  0.7 19.7 %copy-start.12 = (s32[1,32]{1,0:T(1,128)S(1)}, s32[1,32]{1,0:T(1,128)}, u32[]{:S(2)}) copy-start(s32[1,32]{1,0:T(1,128)} %param.14) | copy-start | bytes 388
  0.7 20.2 %copy-start.6 = (s32[4,6]{1,0:T(4,128)S(1)}, s32[4,6]{1,0:T(4,128)}, u32[]{:S(2)}) copy-start(s32[4,6]{1,0:T(4,128)} %param.9) | copy-start | bytes 292
  0.7 22.2 %copy-start.3 = (s32[4,128]{1,0:T(4,128)S(1)}, s32[4,128]{1,0:T(4,128)}, u32[]{:S(2)}) copy-start(s32[4,128]{1,0:T(4,128)} %param.11) | copy-start | bytes 6148
  3.5 23.0 %collective-permute-start.1 = (bf16[768,512]{1,0:T(8,128)(2,1)}, bf16[768,512]{1,0:T(8,128)(2,1)}, u32[]{:S(2)}, u32[]{:S(2)}) collective-permute-start(bf16[768,512]{1,0:T(8,128)(2,1)} %get-tuple-element.8), channel_id=1, source_target_pairs={{1,0},{2,1},{3,2},{4,3},{5,4},{6,5},{7,6},{8,7},{9,8},{10,9},{11,1... | collective-permute-start | bytes 2359304 | tf_op jit(solution)/shard_map/ppermute | solution.py:17
  16.7 17.8 %collective-permute-start = (bf16[768,512]{1,0:T(8,128)(2,1)}, bf16[768,512]{1,0:T(8,128)(2,1)}, u32[]{:S(2)}, u32[]{:S(2)}) collective-permute-start(bf16[768,512]{1,0:T(8,128)(2,1)} %get-tuple-element.7), channel_id=1, source_target_pairs={{0,1},{1,2},{2,3},{3,4},{4,5},{5,6},{6,7},{7,8},{8,9},{9,10},{10,1... | collective-permute-start | bytes 2359304 | tf_op jit(solution)/shard_map/ppermute | solution.py:14
  22.9 39.8 %copy-start.4 = (pred[4,128]{1,0:T(4,128)(4,1)}, pred[4,128]{1,0:T(4,128)(4,1)S(1)}, u32[]{:S(2)}) copy-start(pred[4,128]{1,0:T(4,128)(4,1)S(1)} %compare_and_fusion.3) | copy-start | bytes 1540
  62.7 4.2 %copy-start.1 = (f32[512,512]{1,0:T(8,128)S(1)}, f32[512,512]{1,0:T(8,128)}, u32[]{:S(2)}) copy-start(f32[512,512]{1,0:T(8,128)} %gather_fusion.4) | copy-start | bytes 3145732
  73.8 93.4 %copy-start.5 = (pred[512]{0:T(512)(128)(4,1)S(1)}, pred[512]{0:T(512)(128)(4,1)}, u32[]{:S(2)}) copy-start(pred[512]{0:T(512)(128)(4,1)} %fusion.66) | copy-start | bytes 1540
  163.5 3.6 %copy-start.2 = (f32[512,512]{1,0:T(8,128)S(1)}, f32[512,512]{1,0:T(8,128)}, u32[]{:S(2)}) copy-start(f32[512,512]{1,0:T(8,128)} %gather_fusion.4) | copy-start | bytes 3145732
  165.7 5.5 %copy-start.9 = (pred[128]{0:T(512)(128)(4,1)S(1)}, pred[128]{0:T(512)(128)(4,1)}, u32[]{:S(2)}) copy-start(pred[128]{0:T(512)(128)(4,1)} %compare_and_fusion.2) | copy-start | bytes 388
  168.3 36.8 %copy-start.7 = (pred[64]{0:T(512)(128)(4,1)S(1)}, pred[64]{0:T(512)(128)(4,1)}, u32[]{:S(2)}) copy-start(pred[64]{0:T(512)(128)(4,1)} %compare_and_fusion.1) | copy-start | bytes 196
  171.2 38.1 %copy-start.8 = (pred[32]{0:T(512)(128)(4,1)S(1)}, pred[32]{0:T(512)(128)(4,1)}, u32[]{:S(2)}) copy-start(pred[32]{0:T(512)(128)(4,1)} %compare_and_fusion) | copy-start | bytes 100
  206.1 23.0 %collective-permute-start.2 = (f32[64,512]{1,0:T(8,128)S(1)}, f32[64,512]{1,0:T(8,128)}, u32[]{:S(2)}, u32[]{:S(2)}) collective-permute-start(f32[64,512]{1,0:T(8,128)S(1)} %broadcast_select_fusion.2), channel_id=1, source_target_pairs={{0,1},{1,0},{2,3},{3,2},{4,5},{5,4},{6,7},{7,6},{8,9},{9,8},{10,11... | collective-permute-start | bytes 393224 | tf_op jit(solution)/shard_map/ppermute | solution.py:29
  210.3 6.0 %collective-permute-start.3 = (f32[32,512]{1,0:T(8,128)S(1)}, f32[32,512]{1,0:T(8,128)S(1)}, u32[]{:S(2)}, u32[]{:S(2)}) collective-permute-start(f32[32,512]{1,0:T(8,128)S(1)} %broadcast_select_fusion.3), channel_id=1, source_target_pairs={{0,1},{1,0},{2,3},{3,2},{4,5},{5,4},{6,7},{7,6},{8,9},{9,8},{10,11... | collective-permute-start | bytes 196616 | tf_op jit(solution)/shard_map/ppermute | solution.py:29
  216.9 53.6 %collective-permute-start.4 = (f32[64,512]{1,0:T(8,128)}, f32[64,512]{1,0:T(8,128)}, u32[]{:S(2)}, u32[]{:S(2)}) collective-permute-start(f32[64,512]{1,0:T(8,128)} %maximum_select_fusion.2), channel_id=1, source_target_pairs={{0,2},{2,0},{1,3},{3,1},{4,6},{6,4},{5,7},{7,5},{8,10},{10,8},{9,1... | collective-permute-start | bytes 393224 | tf_op jit(solution)/shard_map/ppermute | solution.py:29
where the time goes:
time: 306 us; the launch traced here: 301 us
  other arithmetic  188 us (61%)
  matrix products  33.9 us (11%)
  local copies, waits for them, and re-layouts  32.5 us (11%)
  starting transfers between devices  31.6 us (10%)
  waiting for transfers between devices  11.1 us (4%)
  between operations  3.12 us (1%)
    another operation x13, other arithmetic, project(): factor = jnp.linalg.cholesky(matrix)  89.5 us
    another operation x9, other arithmetic, project(): lax.linalg.triangular_solve(factor, inner, left_side=True, lower=True, tr...  76.1 us
    ppermute x3, starting transfers between devices, from_partner(): return lax.ppermute(block, axis, route)  16.5 us
    gather x4, local copies, waits for them, and re-layouts, select_rows(): return jnp.take(rows, index, axis=0)  15 us
    ppermute x1, starting transfers between devices, padded_2(): lax.ppermute(lax.slice_in_dim(block, 0, width, axis=dim), axis, backward)  13.2 us
    dot_general x4, matrix products, project(): coupling = jnp.dot(rows, skeleton.T, precision=highest)  10.1 us
    ppermute x1, waiting for transfers between devices, padded_2(): lax.ppermute(lax.slice_in_dim(block, block.shape[dim] - width, None, axis...  8.04 us
    reduce_sum x4, other arithmetic, project(): damping = jnp.sum(skeleton * skeleton) / skeleton.shape[0] + 1e-06  6.67 us
  transfers between devices with their start and end apart: 5, of which 2 were waited for; matrix products, arithmetic and copies ran while one was open for 17% of the time, Pallas kernels for 0%

commit v1 on v0

v1 whole, which is shorter than its diff:
```python
import functools

import jax
import jax.numpy as jnp
from jax import lax
from jax.experimental import pallas as pl
from jax.experimental.pallas import tpu as pltpu
from jax.sharding import PartitionSpec as P

HALF = 3
NNZ = 6
LEAVES = 4
BLOCK = 256
SKEL = 128
COLS = 512
STEPS = 6

F32 = jnp.float32
BF16 = jnp.bfloat16
MESH = pl.DeviceIdType.MESH
NN = (((1,), (0,)), ((), ()))
NT = (((1,), (1,)), ((), ()))


def dot(a, b, dims=NN):
    return lax.dot_general(a, b, dims, preferred_element_type=F32)


def dot_highest(a, b):
    return lax.dot_general(
        a, b, NN, precision=lax.Precision.HIGHEST, preferred_element_type=F32
    )


def split(x):
    high = x.astype(BF16)
    low = (x - high.astype(F32)).astype(BF16)
    return high, low


def eye():
    row = lax.broadcasted_iota(jnp.int32, (SKEL, SKEL), 0)
    col = lax.broadcasted_iota(jnp.int32, (SKEL, SKEL), 1)
    return row == col


def gram(rows_high, rows_low, skel_high, skel_low):
    count = rows_high.shape[0]
    left = jnp.concatenate([rows_high, rows_low], axis=0)
    right = jnp.concatenate([skel_high, skel_low], axis=0)
    full = dot(left, right, NT)
    return (full[:count, :SKEL] + full[count:, :SKEL]) + (
        full[:count, SKEL:] + full[count:, SKEL:]
    )


def normalized(moment):
    diagonal = eye()
    trace = jnp.sum(jnp.where(diagonal, moment, 0.0), keepdims=True)
    damping = trace / SKEL + 1e-06
    scale = 1.0 / (65.0 * damping)
    return (moment + jnp.where(diagonal, damping, 0.0)) * scale, scale


def invert(start_ref, pair_ref, which):
    for j in which:
        high, low = split(start_ref[j])
        identity = jnp.where(eye(), 1.0, 0.0).astype(BF16)
        pair_ref[j, :, 0:128] = high
        pair_ref[j, :, 128:256] = low
        pair_ref[j, :, 256:384] = identity
        pair_ref[j, :, 384:512] = jnp.zeros_like(identity)

    def step(_, rho):
        gain = 2.0 / (2.0 - rho * rho)
        for j in which:
            held = pair_ref[j]
            out = dot(held[:, :256], jnp.concatenate([held, held], axis=0))
            t = held[:, 0:128].astype(F32) + held[:, 128:256].astype(F32)
            x = held[:, 256:384].astype(F32) + held[:, 384:512].astype(F32)
            t = gain * (2.0 * t - (out[:, 0:128] + out[:, 128:256]))
            x = gain * (2.0 * x - (out[:, 256:384] + out[:, 384:512]))
            high, low = split(t)
            pair_ref[j, :, 0:128] = high
            pair_ref[j, :, 128:256] = low
            high, low = split(x)
            pair_ref[j, :, 256:384] = high
            pair_ref[j, :, 384:512] = low
        return gain - 1.0

    lax.fori_loop(0, STEPS, step, jnp.float32(128.0 / 130.0))
    inverses = []
    for j in which:
        held = pair_ref[j]
        x = held[:, 256:384].astype(F32) + held[:, 384:512].astype(F32)
        left = dot_highest(start_ref[j], x)
        rest = jnp.where(eye(), 1.0, 0.0) - left
        inverses.append(x + dot_highest(x, rest))
    return inverses


def kernel(
    quads, tiles,
    offsets_ref, leaf_ref, node_ref, pair_ref, group_ref, blocks_hbm, sketch_hbm,
    leaf_hbm, node_hbm, pairs_hbm, groups_hbm,
    window, mats, pivots, pick_leaf, pick_up, rows, skel, coupling, node_coupling, small_coupling,
    start, work, pair_buf, group_buf, node_skel,
    leaf_out, node_out, pairs_out, groups_out,
    local_sem, send_sem, recv_sem, up_send, up_recv, out_sem,
):
    q = lax.axis_index("quad")
    t = lax.axis_index("tile")
    me = q * tiles + t
    last = quads * tiles - 1
    odd = t % 2
    even = 1 - odd

    def at(flat):
        return (flat // tiles, flat % tiles)

    own = pltpu.make_async_copy(sketch_hbm, window.at[pl.ds(HALF, LEAVES)], local_sem.at[LEAVES])
    own.start()
    loads = [
        pltpu.make_async_copy(blocks_hbm.at[i], mats.at[i], local_sem.at[i]) for i in range(LEAVES)
    ]
    for load in loads:
        load.start()

    sibling = (q, t + 1 - 2 * odd)
    pair_of = t // 2
    other_pair = pair_of + 1 - 2 * (pair_of % 2)
    cousins = [(q, 2 * other_pair), (q, 2 * other_pair + 1)]
    partners = [sibling] + cousins

    barrier = pltpu.get_barrier_semaphore()

    @pl.when(me > 0)
    def _():
        pl.semaphore_signal(barrier, inc=1, device_id=at(me - 1), device_id_type=MESH)

    @pl.when(me < last)
    def _():
        pl.semaphore_signal(barrier, inc=1, device_id=at(me + 1), device_id_type=MESH)

    for partner in partners:
        pl.semaphore_signal(barrier, inc=1, device_id=partner, device_id_type=MESH)
    ends = jnp.where(me > 0, 1, 0) + jnp.where(me < last, 1, 0)
    pl.semaphore_wait(barrier, 3 + ends)

    def to_right(j):
        return pltpu.make_async_remote_copy(
            src_ref=sketch_hbm.at[LEAVES - 1 - j], dst_ref=window.at[HALF - 1 - j],
            send_sem=send_sem.at[j], recv_sem=recv_sem.at[HALF - 1 - j],
            device_id=at(me + 1), device_id_type=MESH,
        )

    def to_left(j):
        return pltpu.make_async_remote_copy(
            src_ref=sketch_hbm.at[j], dst_ref=window.at[HALF + LEAVES + j],
            send_sem=send_sem.at[HALF + j], recv_sem=recv_sem.at[HALF + j],
            device_id=at(me - 1), device_id_type=MESH,
        )

    @pl.when(me < last)
    def _():
        for j in range(HALF):
            to_right(j).start()

    @pl.when(me > 0)
    def _():
        for j in range(HALF):
            to_left(j).start()

    @pl.when(me == 0)
    def _():
        window[0:HALF] = jnp.zeros((HALF, BLOCK, COLS), BF16)

    @pl.when(me == last)
    def _():
        window[HALF + LEAVES:] = jnp.zeros((HALF, BLOCK, COLS), BF16)

    pivots[...] = jnp.full((8, 128), -1.0, F32)
    pivots[0:4, :] = leaf_ref[...].astype(F32)
    pivots[4:5, :] = node_ref[...].astype(F32)
    pivots[5:6, 0:64] = pair_ref[...].astype(F32)
    pivots[6:7, 0:32] = group_ref[...].astype(F32)

    def one_hot(row, width):
        down = jnp.broadcast_to(pivots[row:row + 1, :], (128, 128)).T
        down = jnp.concatenate([down] * (width // 128), axis=1)
        lane = lax.broadcasted_iota(jnp.int32, (128, width), 1).astype(F32)
        return jnp.where(down == lane, 1.0, 0.0).astype(BF16)

    for i in range(LEAVES):
        pick_leaf[i] = one_hot(i, BLOCK)
    node_pick = one_hot(4, LEAVES * SKEL)
    upper_pick = dot(one_hot(5, SKEL)[0:64], node_pick).astype(BF16)
    higher_pick = dot(one_hot(6, 128)[0:32, 0:64], upper_pick).astype(BF16)
    pick_up[0:128] = node_pick
    pick_up[128:192] = upper_pick
    pick_up[192:224] = higher_pick

    own.wait()

    def arrived(slot, index):
        return pltpu.make_async_remote_copy(
            src_ref=window.at[slot], dst_ref=window.at[slot],
            send_sem=send_sem.at[0], recv_sem=recv_sem.at[index],
            device_id=sibling, device_id_type=MESH,
        )

    for j in range(HALF):
        arrived(j + (HALF + LEAVES) * even, j + HALF * even).wait_recv()

    for s in range(LEAVES):
        i = even * (LEAVES - 1 - s) + odd * s
        if s > 0:
            @pl.when((me > 0) & (me < last))
            def _():
                arrived(even * (HALF - s) + odd * (HALF + LEAVES - 1 + s),
                        even * (HALF - s) + odd * (HALF - 1 + s)).wait_recv()
        pltpu.make_async_copy(blocks_hbm.at[i], mats.at[i], local_sem.at[i]).wait()
        total = jnp.zeros((BLOCK, COLS), F32)
        for k in range(NNZ):
            near = offsets_ref[i, k] == k - HALF
            panel = jnp.where(near, window[i + k], window[i + k + 1])
            total = total + dot(mats[i, k], panel)
        high, low = split(total)
        pick = pick_leaf[i]
        skel_high = dot(pick, high).astype(BF16)
        skel_low = dot(pick, low).astype(BF16)
        skel[0, i] = skel_high
        skel[1, i] = skel_low
        matrix, scale = normalized(gram(skel_high, skel_low, skel_high, skel_low))
        start[i] = matrix
        coupling[i] = gram(high, low, skel_high, skel_low) * scale

    all_high = skel[0].reshape(LEAVES * SKEL, COLS)
    all_low = skel[1].reshape(LEAVES * SKEL, COLS)
    up_high = dot(pick_up[...], all_high).astype(BF16)
    up_low = dot(pick_up[...], all_low).astype(BF16)
    place = t % 4
    pair_buf[odd, 0] = up_high[128:192]
    pair_buf[odd, 1] = up_low[128:192]
    group_buf[place, 0] = up_high[192:224]
    group_buf[place, 1] = up_low[192:224]
    node_skel[0] = up_high[0:128]
    node_skel[1] = up_low[0:128]

    sends = [
        pltpu.make_async_remote_copy(
            src_ref=pair_buf.at[odd], dst_ref=pair_buf.at[odd],
            send_sem=up_send.at[0], recv_sem=up_recv.at[0],
            device_id=sibling, device_id_type=MESH,
        )
    ]
    for n, partner in enumerate(partners):
        sends.append(
            pltpu.make_async_remote_copy(
                src_ref=group_buf.at[place], dst_ref=group_buf.at[place],
                send_sem=up_send.at[1 + n], recv_sem=up_recv.at[1 + place],
                device_id=partner, device_id_type=MESH,
            )
        )
    for send in sends:
        send.start()

    node_high = node_skel[0]
    node_low = node_skel[1]
    matrix, scale = normalized(gram(node_high, node_low, node_high, node_low))
    start[LEAVES] = matrix
    node_coupling[...] = gram(all_high, all_low, node_high, node_low) * scale

    inverses = invert(start, work, range(LEAVES + 1))
    for i in range(LEAVES):
        leaf_out[i] = dot_highest(coupling[i], inverses[i])
    node_out[...] = dot_highest(node_coupling[...], inverses[LEAVES])
    puts = [
        pltpu.make_async_copy(leaf_out, leaf_hbm, out_sem.at[0]),
        pltpu.make_async_copy(node_out, node_hbm, out_sem.at[1]),
    ]
    for put in puts:
        put.start()

    pltpu.make_async_remote_copy(
        src_ref=pair_buf.at[even], dst_ref=pair_buf.at[even],
        send_sem=up_send.at[0], recv_sem=up_recv.at[0],
        device_id=sibling, device_id_type=MESH,
    ).wait_recv()
    for n in range(1, 4):
        spot = (place + n) % 4
        pltpu.make_async_remote_copy(
            src_ref=group_buf.at[spot], dst_ref=group_buf.at[spot],
            send_sem=up_send.at[0], recv_sem=up_recv.at[1 + spot],
            device_id=sibling, device_id_type=MESH,
        ).wait_recv()

    pair_high = jnp.concatenate([pair_buf[0, 0], pair_buf[1, 0]], axis=0)
    pair_low = jnp.concatenate([pair_buf[0, 1], pair_buf[1, 1]], axis=0)
    group_high = jnp.concatenate([group_buf[g, 0] for g in range(4)], axis=0)
    group_low = jnp.concatenate([group_buf[g, 1] for g in range(4)], axis=0)
    matrix, scale = normalized(gram(pair_high, pair_low, pair_high, pair_low))
    start[5] = matrix
    small_coupling[0:128] = gram(node_skel[0], node_skel[1], pair_high, pair_low) * scale
    matrix, scale = normalized(gram(group_high, group_low, group_high, group_low))
    start[6] = matrix
    small_coupling[128:192] = gram(pair_buf[odd, 0], pair_buf[odd, 1], group_high, group_low) * scale
    inverses = invert(start, work, (5, 6))
    pairs_out[...] = dot_highest(small_coupling[0:128], inverses[0])
    groups_out[...] = dot_highest(small_coupling[128:192], inverses[1])
    more = [
        pltpu.make_async_copy(pairs_out, pairs_hbm, out_sem.at[2]),
        pltpu.make_async_copy(groups_out, groups_hbm, out_sem.at[3]),
    ]
    for put in more:
        put.start()

    @pl.when(me < last)
    def _():
        for j in range(HALF):
            to_right(j).wait_send()

    @pl.when(me > 0)
    def _():
        for j in range(HALF):
            to_left(j).wait_send()

    for send in sends:
        send.wait_send()
    for put in puts + more:
        put.wait()


def body(quads, tiles, blocks, offsets, sketch, leaf_pivots, node_pivots, pair_pivots, group_pivots):
    any_space = pl.BlockSpec(memory_space=pl.ANY)
    vmem = pl.BlockSpec(memory_space=pltpu.VMEM)
    shapes = [
        ((LEAVES, BLOCK, SKEL), F32),
        ((LEAVES * SKEL, SKEL), F32),
        ((SKEL, SKEL), F32),
        ((SKEL // 2, SKEL), F32),
    ]
    outs = pl.pallas_call(
        functools.partial(kernel, quads, tiles),
        out_shape=[jax.ShapeDtypeStruct(s, d) for s, d in shapes],
        in_specs=[pl.BlockSpec(memory_space=pltpu.SMEM), vmem, vmem, vmem, vmem, any_space, any_space],
        out_specs=[any_space] * 4,
        scratch_shapes=[
            pltpu.VMEM((LEAVES + 2 * HALF, BLOCK, COLS), BF16),
            pltpu.VMEM((LEAVES, NNZ, BLOCK, BLOCK), BF16),
            pltpu.VMEM((8, 128), F32),
            pltpu.VMEM((LEAVES, SKEL, BLOCK), BF16),
            pltpu.VMEM((224, LEAVES * SKEL), BF16),
            pltpu.VMEM((8, 128), F32),
            pltpu.VMEM((2, LEAVES, SKEL, COLS), BF16),
            pltpu.VMEM((LEAVES, BLOCK, SKEL), F32),
            pltpu.VMEM((LEAVES * SKEL, SKEL), F32),
            pltpu.VMEM((192, SKEL), F32),
            pltpu.VMEM((7, SKEL, SKEL), F32),
            pltpu.VMEM((7, SKEL, 4 * SKEL), BF16),
            pltpu.VMEM((2, 2, 64, COLS), BF16),
            pltpu.VMEM((4, 2, 32, COLS), BF16),
            pltpu.VMEM((2, SKEL, COLS), BF16),
            pltpu.VMEM((LEAVES, BLOCK, SKEL), F32),
            pltpu.VMEM((LEAVES * SKEL, SKEL), F32),
            pltpu.VMEM((SKEL, SKEL), F32),
            pltpu.VMEM((SKEL // 2, SKEL), F32),
            pltpu.SemaphoreType.DMA((LEAVES + 1,)),
            pltpu.SemaphoreType.DMA((2 * HALF,)),
            pltpu.SemaphoreType.DMA((2 * HALF,)),
            pltpu.SemaphoreType.DMA((4,)),
            pltpu.SemaphoreType.DMA((5,)),
            pltpu.SemaphoreType.DMA((4,)),
        ],
        compiler_params=pltpu.CompilerParams(collective_id=0, has_side_effects=True),
        name="compress",
    )(offsets, leaf_pivots, node_pivots, pair_pivots, group_pivots,
      blocks, sketch.reshape(LEAVES, BLOCK, COLS))
    return outs[0].reshape(LEAVES * BLOCK, SKEL), outs[1], outs[2], outs[3]


def solution(mesh):
    split_all = P(("quad", "tile"), None)
    placed = (P(("quad", "tile"), None, None, None),) + (split_all,) * 6
    run = functools.partial(body, mesh.shape["quad"], mesh.shape["tile"])
    return jax.shard_map(
        run, mesh=mesh, in_specs=placed, out_specs=(split_all,) * 4, check_vma=False
    )
```

time: 306 us -> 41.8 us (0.14); the launches traced: 301 us -> 41.4 us
  other arithmetic: 188 us -> 0 us
  Pallas kernels: 0 us -> 34.4 us
  matrix products: 33.9 us -> 0 us
  starting transfers between devices: 31.6 us -> 0 us
  local copies, waits for them, and re-layouts: 32.5 us -> 6.38 us
  waiting for transfers between devices: 11.1 us -> 0 us
    another operation x22 -> x0, other arithmetic: 166 us -> none  [the longest x13 89.5 us: project(): factor = jnp.linalg.cholesky(matrix)]
    pallas_call x0 -> x1, Pallas kernels: none -> 34.4 us  [body(): pl.pallas_call(functools.partial(kernel, quads, tiles), out_shape=[jax.Sh...]
    ppermute x5 -> x0, starting transfers between devices: 31.6 us -> none  [the longest x3 16.5 us: from_partner(): return lax.ppermute(block, axis, route)]
    dot_general x9 -> x0, matrix products: 22.8 us -> none  [the longest x4 10.1 us: project(): coupling = jnp.dot(rows, skeleton.T, precision=highest)]
    gather x5 -> x0, local copies, waits for them, and re-layouts: 21.1 us -> none  [the longest x4 15 us: select_rows(): return jnp.take(rows, index, axis=0)]
    another operation x8 -> x0, matrix products: 11.2 us -> none  [the longest x4 6.19 us: project(): lax.linalg.triangular_solve(factor, inner, left_side=True, lower=True, tr...]
    ppermute x5 -> x0, waiting for transfers between devices: 11.1 us -> none  [the longest x1 8.04 us: padded_2(): lax.ppermute(lax.slice_in_dim(block, block.shape[dim] - width, None, axis...]
    reduce_sum x4 -> x0, other arithmetic: 6.67 us -> none  [project(): damping = jnp.sum(skeleton * skeleton) / skeleton.shape[0] + 1e-06]
  transfers between devices with their start and end apart: 5 -> 0, of which waited for: 2 -> 0; matrix products, arithmetic and copies ran while one was open for 17% -> 0% of each run, Pallas kernels for 0% -> 0%
where the time goes in v1:
time: 41.8 us; the launch traced here: 41.4 us
  Pallas kernels  34.4 us (82%)
  local copies, waits for them, and re-layouts  6.38 us (15%)
  between operations  0.64 us (2%)
    pallas_call x1, Pallas kernels, body(): pl.pallas_call(functools.partial(kernel, quads, tiles), out_shape=[jax.Sh...  34.4 us
    unnamed x4, local copies, waits for them, and re-layouts  6.38 us

profile of v1, /device:TPU:24, one launch (start us, length us, event | category | flops | bytes accessed | tf_op | source)
XLA Modules:
  0.0 41.4 jit_solution(2910618271560488779)
XLA Ops:
  0.6 34.4 %compress.1 = (f32[4,256,128]{2,1,0:T(8,128)}, f32[512,128]{1,0:T(8,128)}, f32[128,128]{1,0:T(8,128)}, f32[64,128]{1,0:T(8,128)}) custom-call(s32[4,6]{1,0:T(4,128)} %offsets_ref.1, s32[4,128]{1,0:T(4,128)} %leaf_ref.1, s32[1,128]{1,0:T(1,128)} %node_ref.1, s32[1,64]{1,0:T(1,128)} %pair_ref.1, s32[1,32]{1,0:T(1,128)} %group_ref.1, ...), custom_call_target="tpu_custom_call" | custom-call | tf_op jit(solution)/shard_map/compress/pallas_call | solution.py:343
  35.0 1.9 %copy.15 = f32[1024,128]{1,0:T(8,128)} copy(f32[1024,128]{1,0:T(8,128)} %bitcast.3) | data formatting | bytes 1048576
  36.9 1.7 %copy.16 = f32[512,128]{1,0:T(8,128)} copy(f32[512,128]{1,0:T(8,128)} %get-tuple-element.17) | data formatting | bytes 524288
  38.6 1.5 %copy.17 = f32[128,128]{1,0:T(8,128)} copy(f32[128,128]{1,0:T(8,128)} %get-tuple-element.18) | data formatting | bytes 131072
  40.1 1.4 %copy.18 = f32[64,128]{1,0:T(8,128)} copy(f32[64,128]{1,0:T(8,128)} %get-tuple-element.19) | data formatting | bytes 65536

commit v2 on v1

v2 whole, which is shorter than its diff:
```python
import functools

import jax
import jax.numpy as jnp
from jax import lax
from jax.experimental import pallas as pl
from jax.experimental.pallas import tpu as pltpu
from jax.sharding import PartitionSpec as P

HALF = 3
NNZ = 6
LEAVES = 4
BLOCK = 256
SKEL = 128
COLS = 512
STEPS = 6

F32 = jnp.float32
BF16 = jnp.bfloat16
MESH = pl.DeviceIdType.MESH
NN = (((1,), (0,)), ((), ()))
NT = (((1,), (1,)), ((), ()))


def dot(a, b, dims=NN):
    return lax.dot_general(a, b, dims, preferred_element_type=F32)


def dot_highest(a, b):
    return lax.dot_general(
        a, b, NN, precision=lax.Precision.HIGHEST, preferred_element_type=F32
    )


def split(x):
    high = x.astype(BF16)
    low = (x - high.astype(F32)).astype(BF16)
    return high, low


def eye():
    row = lax.broadcasted_iota(jnp.int32, (SKEL, SKEL), 0)
    col = lax.broadcasted_iota(jnp.int32, (SKEL, SKEL), 1)
    return row == col


def gram(rows_high, rows_low, skel_high, skel_low):
    count = rows_high.shape[0]
    left = jnp.concatenate([rows_high, rows_low], axis=0)
    right = jnp.concatenate([skel_high, skel_low], axis=0)
    full = dot(left, right, NT)
    return (full[:count, :SKEL] + full[count:, :SKEL]) + (
        full[:count, SKEL:] + full[count:, SKEL:]
    )


def normalized(moment):
    diagonal = eye()
    trace = jnp.sum(jnp.where(diagonal, moment, 0.0), keepdims=True)
    damping = trace / SKEL + 1e-06
    scale = 1.0 / (65.0 * damping)
    return (moment + jnp.where(diagonal, damping, 0.0)) * scale, scale


def invert(start_ref, pair_ref, which):
    for j in which:
        high, low = split(start_ref[j])
        identity = jnp.where(eye(), 1.0, 0.0).astype(BF16)
        pair_ref[j, :, 0:128] = high
        pair_ref[j, :, 128:256] = low
        pair_ref[j, :, 256:384] = identity
        pair_ref[j, :, 384:512] = jnp.zeros_like(identity)

    def step(_, rho):
        gain = 2.0 / (2.0 - rho * rho)
        for j in which:
            held = pair_ref[j]
            out = dot(held[:, :256], jnp.concatenate([held, held], axis=0))
            t = held[:, 0:128].astype(F32) + held[:, 128:256].astype(F32)
            x = held[:, 256:384].astype(F32) + held[:, 384:512].astype(F32)
            t = gain * (2.0 * t - (out[:, 0:128] + out[:, 128:256]))
            x = gain * (2.0 * x - (out[:, 256:384] + out[:, 384:512]))
            high, low = split(t)
            pair_ref[j, :, 0:128] = high
            pair_ref[j, :, 128:256] = low
            high, low = split(x)
            pair_ref[j, :, 256:384] = high
            pair_ref[j, :, 384:512] = low
        return gain - 1.0

    lax.fori_loop(0, STEPS, step, jnp.float32(128.0 / 130.0))
    inverses = []
    for j in which:
        held = pair_ref[j]
        x = held[:, 256:384].astype(F32) + held[:, 384:512].astype(F32)
        left = dot_highest(start_ref[j], x)
        rest = jnp.where(eye(), 1.0, 0.0) - left
        inverses.append(x + dot_highest(x, rest))
    return inverses


def kernel(
    quads, tiles,
    offsets_hbm, leaf_hbm, node_hbm, pair_hbm, group_hbm, blocks_hbm, sketch_hbm,
    leaf_result, node_result, node_rows, pair_rows, group_rows,
    window, mats, offsets, leaf_index, node_index, pair_index, group_index, pivots, pick_leaf, pick_up, pick_send, partial,
    skel, coupling, node_coupling, start, work, upper, higher, node_skel,
    leaf_out, node_out,
    local_sem, index_sem, send_sem, recv_sem, up_send, up_recv, out_sem,
):
    q = lax.axis_index("quad")
    t = lax.axis_index("tile")
    me = q * tiles + t
    last = quads * tiles - 1
    odd = t % 2
    even = 1 - odd

    def at(flat):
        return (flat // tiles, flat % tiles)

    sibling = (q, t + 1 - 2 * odd)
    pair_of = t // 2
    other_pair = pair_of + 1 - 2 * (pair_of % 2)
    cousins = [(q, 2 * other_pair), (q, 2 * other_pair + 1)]
    partners = cousins + [sibling]

    barrier = pltpu.get_barrier_semaphore()

    @pl.when(me > 0)
    def _():
        pl.semaphore_signal(barrier, inc=1, device_id=at(me - 1), device_id_type=MESH)

    @pl.when(me < last)
    def _():
        pl.semaphore_signal(barrier, inc=1, device_id=at(me + 1), device_id_type=MESH)

    for partner in partners:
        pl.semaphore_signal(barrier, inc=1, device_id=partner, device_id_type=MESH)

    smalls = [
        pltpu.make_async_copy(offsets_hbm, offsets, index_sem.at[0]),
        pltpu.make_async_copy(leaf_hbm, leaf_index, index_sem.at[1]),
        pltpu.make_async_copy(node_hbm, node_index, index_sem.at[2]),
        pltpu.make_async_copy(pair_hbm, pair_index, index_sem.at[3]),
        pltpu.make_async_copy(group_hbm, group_index, index_sem.at[4]),
    ]
    for small in smalls:
        small.start()
    own = pltpu.make_async_copy(sketch_hbm, window.at[pl.ds(HALF, LEAVES)], local_sem.at[LEAVES])
    own.start()

    def leaf_at(s):
        return even * (LEAVES - 1 - s) + odd * s

    def load(i):
        return pltpu.make_async_copy(blocks_hbm.at[i], mats.at[i], local_sem.at[i])

    for s in range(LEAVES):
        load(leaf_at(s)).start()

    ends = jnp.where(me > 0, 1, 0) + jnp.where(me < last, 1, 0)
    pl.semaphore_wait(barrier, 3 + ends)

    def to_right(j):
        return pltpu.make_async_remote_copy(
            src_ref=sketch_hbm.at[LEAVES - 1 - j], dst_ref=window.at[HALF - 1 - j],
            send_sem=send_sem.at[j], recv_sem=recv_sem.at[HALF - 1 - j],
            device_id=at(me + 1), device_id_type=MESH,
        )

    def to_left(j):
        return pltpu.make_async_remote_copy(
            src_ref=sketch_hbm.at[j], dst_ref=window.at[HALF + LEAVES + j],
            send_sem=send_sem.at[HALF + j], recv_sem=recv_sem.at[HALF + j],
            device_id=at(me - 1), device_id_type=MESH,
        )

    @pl.when(me < last)
    def _():
        for j in range(HALF):
            to_right(j).start()

    @pl.when(me > 0)
    def _():
        for j in range(HALF):
            to_left(j).start()

    @pl.when(me == 0)
    def _():
        window[0:HALF] = jnp.zeros((HALF, BLOCK, COLS), BF16)

    @pl.when(me == last)
    def _():
        window[HALF + LEAVES:] = jnp.zeros((HALF, BLOCK, COLS), BF16)

    for small in smalls:
        small.wait()
    pivots[...] = jnp.full((8, 128), -1.0, F32)
    pivots[0:4, :] = leaf_index[...].astype(F32)
    pivots[4:5, :] = node_index[...].astype(F32)
    pivots[5:6, 0:64] = pair_index[...].astype(F32)
    pivots[6:7, 0:32] = group_index[...].astype(F32)

    def one_hot(row, width):
        down = jnp.broadcast_to(pivots[row:row + 1, :], (128, 128)).T
        down = jnp.concatenate([down] * (width // 128), axis=1)
        lane = lax.broadcasted_iota(jnp.int32, (128, width), 1).astype(F32)
        return jnp.where(down == lane, 1.0, 0.0).astype(BF16)

    for i in range(LEAVES):
        pick_leaf[i] = one_hot(i, BLOCK)
    node_pick = one_hot(4, LEAVES * SKEL)
    upper_pick = dot(one_hot(5, SKEL)[0:64], node_pick).astype(BF16)
    higher_pick = dot(one_hot(6, 128)[0:32, 0:64], upper_pick).astype(BF16)
    pick_up[...] = node_pick
    both_pick = jnp.concatenate([upper_pick, higher_pick], axis=0)
    for i in range(LEAVES):
        pick_send[i] = dot(both_pick[:, i * SKEL:(i + 1) * SKEL], pick_leaf[i]).astype(BF16)
    partial[...] = jnp.zeros_like(partial)

    own.wait()

    def arrived(slot, which):
        return pltpu.make_async_remote_copy(
            src_ref=window.at[slot], dst_ref=window.at[slot],
            send_sem=send_sem.at[0], recv_sem=recv_sem.at[which],
            device_id=sibling, device_id_type=MESH,
        )

    for j in range(HALF):
        arrived(j + (HALF + LEAVES) * even, j + HALF * even).wait_recv()

    def term(i, j):
        k = even * (NNZ - 1 - j) + odd * j
        near = offsets[i, k] == k - HALF
        panel = jnp.where(near, window[i + k], window[i + k + 1])
        return dot(mats[i, k], panel)

    def first_terms(i):
        load(i).wait()
        total = term(i, 0)
        for j in range(1, NNZ - 1):
            total = total + term(i, j)
        return total

    def last_term(s, i, total):
        if s > 0:
            @pl.when((me > 0) & (me < last))
            def _():
                arrived(even * (HALF - s) + odd * (HALF + LEAVES - 1 + s),
                        even * (HALF - s) + odd * (HALF - 1 + s)).wait_recv()
        high, low = split(total + term(i, NNZ - 1))
        partial[0] += dot(pick_send[i], high)
        partial[1] += dot(pick_send[i], low)
        return high, low

    def leaf_stage(s, i, high, low):
        pick = pick_leaf[i]
        skel_high = dot(pick, high).astype(BF16)
        skel_low = dot(pick, low).astype(BF16)
        skel[0, i] = skel_high
        skel[1, i] = skel_low
        matrix, scale = normalized(gram(skel_high, skel_low, skel_high, skel_low))
        start[s] = matrix
        coupling[s] = gram(high, low, skel_high, skel_low) * scale

    def leaf_put(i):
        return pltpu.make_async_copy(leaf_out.at[i], leaf_result.at[i], out_sem.at[i])

    for s in range(LEAVES - 1):
        i = leaf_at(s)
        high, low = last_term(s, i, first_terms(i))
        leaf_stage(s, i, high, low)

    inverses = invert(start, work, range(LEAVES - 1))
    for s in range(LEAVES - 1):
        i = leaf_at(s)
        leaf_out[i] = dot_highest(coupling[s], inverses[s])
        leaf_put(i).start()

    s = LEAVES - 1
    i = leaf_at(s)
    high, low = last_term(s, i, first_terms(i))
    place = t % 4
    upper[0] = partial[0, 0:64].astype(BF16)
    upper[1] = partial[1, 0:64].astype(BF16)
    higher[0] = partial[0, 64:96].astype(BF16)
    higher[1] = partial[1, 64:96].astype(BF16)

    sends = []
    for n, partner in enumerate(partners):
        sends.append(
            pltpu.make_async_remote_copy(
                src_ref=higher, dst_ref=group_rows.at[place],
                send_sem=up_send.at[1 + n], recv_sem=up_recv.at[1 + place],
                device_id=partner, device_id_type=MESH,
            )
        )
    sends.append(
        pltpu.make_async_remote_copy(
            src_ref=upper, dst_ref=pair_rows.at[odd],
            send_sem=up_send.at[0], recv_sem=up_recv.at[0],
            device_id=sibling, device_id_type=MESH,
        )
    )
    for send in sends:
        send.start()
    keeps = [
        pltpu.make_async_copy(upper, pair_rows.at[odd], out_sem.at[5]),
        pltpu.make_async_copy(higher, group_rows.at[place], out_sem.at[6]),
    ]
    for keep in keeps:
        keep.start()

    leaf_stage(s, i, high, low)
    all_high = skel[0].reshape(LEAVES * SKEL, COLS)
    all_low = skel[1].reshape(LEAVES * SKEL, COLS)
    node_high = dot(pick_up[...], all_high).astype(BF16)
    node_low = dot(pick_up[...], all_low).astype(BF16)
    node_skel[0] = node_high
    node_skel[1] = node_low
    keeps.append(pltpu.make_async_copy(node_skel, node_rows, out_sem.at[7]))
    keeps[-1].start()
    matrix, scale = normalized(gram(node_high, node_low, node_high, node_low))
    start[LEAVES] = matrix
    node_coupling[...] = gram(all_high, all_low, node_high, node_low) * scale
    inverses = invert(start, work, (LEAVES - 1, LEAVES))
    leaf_out[i] = dot_highest(coupling[s], inverses[0])
    leaf_put(i).start()
    node_out[...] = dot_highest(node_coupling[...], inverses[1])
    keeps.append(pltpu.make_async_copy(node_out, node_result, out_sem.at[4]))
    keeps[-1].start()

    pltpu.make_async_remote_copy(
        src_ref=upper, dst_ref=pair_rows.at[even],
        send_sem=up_send.at[0], recv_sem=up_recv.at[0],
        device_id=sibling, device_id_type=MESH,
    ).wait_recv()
    for n in range(1, 4):
        spot = (place + n) % 4
        pltpu.make_async_remote_copy(
            src_ref=higher, dst_ref=group_rows.at[spot],
            send_sem=up_send.at[0], recv_sem=up_recv.at[1 + spot],
            device_id=sibling, device_id_type=MESH,
        ).wait_recv()

    @pl.when(me < last)
    def _():
        for j in range(HALF):
            to_right(j).wait_send()

    @pl.when(me > 0)
    def _():
        for j in range(HALF):
            to_left(j).wait_send()

    for send in sends:
        send.wait_send()
    for keep in keeps:
        keep.wait()
    for i in range(LEAVES):
        leaf_put(i).wait()


def finish(
    node_rows, pair_rows, group_rows, leaf_result, node_result,
    leaf_hbm, node_hbm, pairs_hbm, groups_hbm,
    node_skel, pair_buf, group_buf, leaf_out, node_out, small_coupling, start, work,
    pairs_out, groups_out, in_sem, out_sem,
):
    gets = [
        pltpu.make_async_copy(group_rows, group_buf, in_sem.at[0]),
        pltpu.make_async_copy(pair_rows, pair_buf, in_sem.at[1]),
        pltpu.make_async_copy(node_rows, node_skel, in_sem.at[2]),
        pltpu.make_async_copy(leaf_result, leaf_out, in_sem.at[3]),
        pltpu.make_async_copy(node_result, node_out, in_sem.at[4]),
    ]
    for get in gets:
        get.start()
    odd = lax.axis_index("tile") % 2
    gets[0].wait()
    group_high = jnp.concatenate([group_buf[g, 0] for g in range(4)], axis=0)
    group_low = jnp.concatenate([group_buf[g, 1] for g in range(4)], axis=0)
    matrix, scale = normalized(gram(group_high, group_low, group_high, group_low))
    start[1] = matrix
    gets[1].wait()
    pair_high = jnp.concatenate([pair_buf[0, 0], pair_buf[1, 0]], axis=0)
    pair_low = jnp.concatenate([pair_buf[0, 1], pair_buf[1, 1]], axis=0)
    small_coupling[128:192] = gram(pair_buf[odd, 0], pair_buf[odd, 1], group_high, group_low) * scale
    matrix, scale = normalized(gram(pair_high, pair_low, pair_high, pair_low))
    start[0] = matrix
    gets[2].wait()
    small_coupling[0:128] = gram(node_skel[0], node_skel[1], pair_high, pair_low) * scale
    gets[3].wait()
    gets[4].wait()
    puts = [
        pltpu.make_async_copy(leaf_out, leaf_hbm, out_sem.at[0]),
        pltpu.make_async_copy(node_out, node_hbm, out_sem.at[1]),
        pltpu.make_async_copy(pairs_out, pairs_hbm, out_sem.at[2]),
        pltpu.make_async_copy(groups_out, groups_hbm, out_sem.at[3]),
    ]
    puts[0].start()
    puts[1].start()
    inverses = invert(start, work, (0, 1))
    pairs_out[...] = dot_highest(small_coupling[0:128], inverses[0])
    puts[2].start()
    groups_out[...] = dot_highest(small_coupling[128:192], inverses[1])
    puts[3].start()
    for put in puts:
        put.wait()


def body(quads, tiles, blocks, offsets, sketch, leaf_pivots, node_pivots, pair_pivots, group_pivots):
    any_space = pl.BlockSpec(memory_space=pl.ANY)
    dma = pltpu.SemaphoreType.DMA
    leaf_shape = ((LEAVES, BLOCK, SKEL), F32)
    node_shape = ((LEAVES * SKEL, SKEL), F32)
    rows_shape = ((2, SKEL, COLS), BF16)
    pair_shape = ((2, 2, SKEL // 2, COLS), BF16)
    group_shape = ((4, 2, SKEL // 4, COLS), BF16)
    shapes = [leaf_shape, node_shape, rows_shape, pair_shape, group_shape]
    leaf_result, node_result, node_rows, pair_rows, group_rows = pl.pallas_call(
        functools.partial(kernel, quads, tiles),
        out_shape=[jax.ShapeDtypeStruct(s, d) for s, d in shapes],
        in_specs=[any_space] * 7,
        out_specs=[any_space] * 5,
        scratch_shapes=[
            pltpu.VMEM((LEAVES + 2 * HALF, BLOCK, COLS), BF16),
            pltpu.VMEM((LEAVES, NNZ, BLOCK, BLOCK), BF16),
            pltpu.SMEM((LEAVES, NNZ), jnp.int32),
            pltpu.VMEM((LEAVES, 128), jnp.int32),
            pltpu.VMEM((1, 128), jnp.int32),
            pltpu.VMEM((1, 64), jnp.int32),
            pltpu.VMEM((1, 32), jnp.int32),
            pltpu.VMEM((8, 128), F32),
            pltpu.VMEM((LEAVES, SKEL, BLOCK), BF16),
            pltpu.VMEM((SKEL, LEAVES * SKEL), BF16),
            pltpu.VMEM((LEAVES, 96, BLOCK), BF16),
            pltpu.VMEM((2, 96, COLS), F32),
            pltpu.VMEM((2, LEAVES, SKEL, COLS), BF16),
            pltpu.VMEM((LEAVES, BLOCK, SKEL), F32),
            pltpu.VMEM((LEAVES * SKEL, SKEL), F32),
            pltpu.VMEM((LEAVES + 1, SKEL, SKEL), F32),
            pltpu.VMEM((LEAVES + 1, SKEL, 4 * SKEL), BF16),
            pltpu.VMEM((2, SKEL // 2, COLS), BF16),
            pltpu.VMEM((2, SKEL // 4, COLS), BF16),
            pltpu.VMEM(*rows_shape),
            pltpu.VMEM(*leaf_shape),
            pltpu.VMEM(*node_shape),
            dma((LEAVES + 1,)), dma((5,)), dma((2 * HALF,)), dma((2 * HALF,)),
            dma((4,)), dma((5,)), dma((8,)),
        ],
        compiler_params=pltpu.CompilerParams(collective_id=0, has_side_effects=True),
        name="compress",
    )(offsets, leaf_pivots, node_pivots, pair_pivots, group_pivots,
      blocks, sketch.reshape(LEAVES, BLOCK, COLS))
    outs = [leaf_shape, node_shape, ((SKEL, SKEL), F32), ((SKEL // 2, SKEL), F32)]
    leaf, node, pairs, groups = pl.pallas_call(
        finish,
        out_shape=[jax.ShapeDtypeStruct(s, d) for s, d in outs],
        in_specs=[any_space] * 5,
        out_specs=[any_space] * 4,
        scratch_shapes=[
            pltpu.VMEM(*rows_shape),
            pltpu.VMEM(*pair_shape),
            pltpu.VMEM(*group_shape),
            pltpu.VMEM(*leaf_shape),
            pltpu.VMEM(*node_shape),
            pltpu.VMEM((192, SKEL), F32),
            pltpu.VMEM((2, SKEL, SKEL), F32),
            pltpu.VMEM((2, SKEL, 4 * SKEL), BF16),
            pltpu.VMEM((SKEL, SKEL), F32),
            pltpu.VMEM((SKEL // 2, SKEL), F32),
            dma((5,)), dma((4,)),
        ],
        name="finish",
    )(node_rows, pair_rows, group_rows, leaf_result, node_result)
    return leaf.reshape(LEAVES * BLOCK, SKEL), node, pairs, groups


def solution(mesh):
    split_all = P(("quad", "tile"), None)
    placed = (P(("quad", "tile"), None, None, None),) + (split_all,) * 6
    run = functools.partial(body, mesh.shape["quad"], mesh.shape["tile"])
    return jax.shard_map(
        run, mesh=mesh, in_specs=placed, out_specs=(split_all,) * 4, check_vma=False
    )
```

time: 41.8 us -> 36.4 us (0.87)
  local copies, waits for them, and re-layouts: 6.38 us -> 0 us
  Pallas kernels: 34.4 us -> 35.6 us
    unnamed x4 -> x0, local copies, waits for them, and re-layouts: 6.38 us -> none
    pallas_call x0 -> x1, Pallas kernels: none -> 5.16 us  [body(): pl.pallas_call(finish, out_shape=[jax.ShapeDtypeStruct(s, d) for s, d in...]
    pallas_call x1, Pallas kernels: 34.4 us -> 30.4 us  [body(): pl.pallas_call(functools.partial(kernel, quads, tiles), out_shape=[jax.Sh...]
where the time goes in v2:
time: 36.4 us; the launch traced here: 36.2 us
  Pallas kernels  35.6 us (98%)
  between operations  0.64 us (2%)
    pallas_call x1, Pallas kernels, body(): pl.pallas_call(functools.partial(kernel, quads, tiles), out_shape=[jax.Sh...  30.4 us
    pallas_call x1, Pallas kernels, body(): pl.pallas_call(finish, out_shape=[jax.ShapeDtypeStruct(s, d) for s, d in...  5.16 us

profile of v2, /device:TPU:24, one launch (start us, length us, event | category | flops | bytes accessed | tf_op | source)
XLA Modules:
  0.0 36.2 jit_solution(16036778957476722956)
XLA Ops:
  0.6 30.4 %compress.1 = (f32[4,256,128]{2,1,0:T(8,128)}, f32[512,128]{1,0:T(8,128)}, bf16[2,128,512]{2,1,0:T(8,128)(2,1)}, bf16[2,2,64,512]{3,2,1,0:T(8,128)(2,1)}, bf16[4,2,32,512]{3,2,1,0:T(8,128)(2,1)}) custom-call(s32[4,6]{1,0:T(4,128)} %offsets_hbm.1, s32[4,128]{1,0:T(4,128)} %leaf_hbm.1, s32[1,128]{1,0:T(1,128)} %node_hbm.1, s32[1,64]{1,0:T(1,128)} %pair_hbm.1, ...), custom_call_target="tpu_custom_call" | custom-call | tf_op jit(solution)/shard_map/compress/pallas_call | solution.py:422
  31.1 5.2 %finish.1 = (f32[4,256,128]{2,1,0:T(8,128)}, f32[512,128]{1,0:T(8,128)}, f32[128,128]{1,0:T(8,128)}, f32[64,128]{1,0:T(8,128)}) custom-call(bf16[2,128,512]{2,1,0:T(8,128)(2,1)} %get-tuple-element.13.node_rows, bf16[2,2,64,512]{3,2,1,0:T(8,128)(2,1)} %get-tuple-element.14.pair_rows, bf16[4,2,32,512]{3,2,1,0:T(8,128)(2,1)} %get-tuple-element.15.group_rows, ...), custom_call_target="tpu_custom_call" | custom-call | tf_op jit(solution)/shard_map/finish/pallas_call | solution.py:458

commit v3 on v2

--- a/solution.py
+++ b/solution.py
@@ -24,12 +24,6 @@
 
 def dot(a, b, dims=NN):
     return lax.dot_general(a, b, dims, preferred_element_type=F32)
-
-
-def dot_highest(a, b):
-    return lax.dot_general(
-        a, b, NN, precision=lax.Precision.HIGHEST, preferred_element_type=F32
-    )
 
 
 def split(x):
@@ -62,41 +56,61 @@
     return (moment + jnp.where(diagonal, damping, 0.0)) * scale, scale
 
 
-def invert(start_ref, pair_ref, which):
-    for j in which:
-        high, low = split(start_ref[j])
-        identity = jnp.where(eye(), 1.0, 0.0).astype(BF16)
-        pair_ref[j, :, 0:128] = high
-        pair_ref[j, :, 128:256] = low
-        pair_ref[j, :, 256:384] = identity
-        pair_ref[j, :, 384:512] = jnp.zeros_like(identity)
-
-    def step(_, rho):
+def split3(x):
+    high = x.astype(BF16)
+    rest = x - high.astype(F32)
+    middle = rest.astype(BF16)
+    low = (rest - middle.astype(F32)).astype(BF16)
+    return high, middle, low
+
+
+def across(parts):
+    return jnp.concatenate(parts, axis=1)
+
+
+def down(parts):
+    return jnp.concatenate(parts, axis=0)
+
+
+def invert(matrices):
+    unit = jnp.where(eye(), 1.0, 0.0)
+    rho = 128.0 / 130.0
+    ts = list(matrices)
+    xs = [None] * len(ts)
+    for step in range(STEPS):
         gain = 2.0 / (2.0 - rho * rho)
-        for j in which:
-            held = pair_ref[j]
-            out = dot(held[:, :256], jnp.concatenate([held, held], axis=0))
-            t = held[:, 0:128].astype(F32) + held[:, 128:256].astype(F32)
-            x = held[:, 256:384].astype(F32) + held[:, 384:512].astype(F32)
-            t = gain * (2.0 * t - (out[:, 0:128] + out[:, 128:256]))
-            x = gain * (2.0 * x - (out[:, 256:384] + out[:, 384:512]))
-            high, low = split(t)
-            pair_ref[j, :, 0:128] = high
-            pair_ref[j, :, 128:256] = low
-            high, low = split(x)
-            pair_ref[j, :, 256:384] = high
-            pair_ref[j, :, 384:512] = low
-        return gain - 1.0
-
-    lax.fori_loop(0, STEPS, step, jnp.float32(128.0 / 130.0))
+        rho = gain - 1.0
+        for j, t in enumerate(ts):
+            th, tl = split(t)
+            left = across([th, tl, th])
+            if step == 0:
+                square = dot(left, down([th, th, tl]))
+                xs[j] = gain * (2.0 * unit - t)
+                ts[j] = gain * (2.0 * t - square)
+                continue
+            xh, xl = split(xs[j])
+            if step == STEPS - 1:
+                product = dot(left, down([xh, xh, xl]))
+            else:
+                both = dot(left, down([across([th, xh]), across([th, xh]), across([tl, xl])]))
+                ts[j] = gain * (2.0 * t - both[:, :SKEL])
+                product = both[:, SKEL:]
+            xs[j] = gain * (2.0 * xs[j] - product)
     inverses = []
-    for j in which:
-        held = pair_ref[j]
-        x = held[:, 256:384].astype(F32) + held[:, 384:512].astype(F32)
-        left = dot_highest(start_ref[j], x)
-        rest = jnp.where(eye(), 1.0, 0.0) - left
-        inverses.append(x + dot_highest(x, rest))
+    for x, matrix in zip(xs, matrices):
+        xh, xl = split(x)
+        high, middle, low = split3(matrix)
+        near = dot(across([high, middle, high, middle, low]), down([xh, xh, xl, xl, xh]))
+        eh, el = split(unit - near)
+        fix = dot(across([xh, xl, xh]), down([eh, eh, el]))
+        inverses.append((xh.astype(F32) + xl.astype(F32)) + fix)
     return inverses
+
+
+def apply(rows, inverse):
+    rh, rm, rl = split3(rows)
+    xh, xm, xl = split3(inverse)
+    return dot(across([rh, rh, rh, rm, rm, rl]), down([xh, xm, xl, xh, xm, xh]))
 
 
 def kernel(
@@ -104,9 +118,8 @@
     offsets_hbm, leaf_hbm, node_hbm, pair_hbm, group_hbm, blocks_hbm, sketch_hbm,
     leaf_result, node_result, node_rows, pair_rows, group_rows,
     window, mats, offsets, leaf_index, node_index, pair_index, group_index, pivots, pick_leaf, pick_up, pick_send, partial,
-    skel, coupling, node_coupling, start, work, upper, higher, node_skel,
-    leaf_out, node_out,
-    local_sem, index_sem, send_sem, recv_sem, up_send, up_recv, out_sem,
+    skel, coupling, node_coupling, start,
+    local_sem, index_sem, send_sem, recv_sem, up_send, up_recv,
 ):
     q = lax.axis_index("quad")
     t = lax.axis_index("tile")
@@ -264,82 +277,64 @@
         start[s] = matrix
         coupling[s] = gram(high, low, skel_high, skel_low) * scale
 
-    def leaf_put(i):
-        return pltpu.make_async_copy(leaf_out.at[i], leaf_result.at[i], out_sem.at[i])
-
     for s in range(LEAVES - 1):
         i = leaf_at(s)
         high, low = last_term(s, i, first_terms(i))
         leaf_stage(s, i, high, low)
 
-    inverses = invert(start, work, range(LEAVES - 1))
+    inverses = invert([start[s] for s in range(LEAVES - 1)])
     for s in range(LEAVES - 1):
         i = leaf_at(s)
-        leaf_out[i] = dot_highest(coupling[s], inverses[s])
-        leaf_put(i).start()
+        leaf_result[i] = apply(coupling[s], inverses[s])
 
     s = LEAVES - 1
     i = leaf_at(s)
     high, low = last_term(s, i, first_terms(i))
     place = t % 4
-    upper[0] = partial[0, 0:64].astype(BF16)
-    upper[1] = partial[1, 0:64].astype(BF16)
-    higher[0] = partial[0, 64:96].astype(BF16)
-    higher[1] = partial[1, 64:96].astype(BF16)
+    for part in range(2):
+        pair_rows[odd, part] = partial[part, 0:64].astype(BF16)
+        group_rows[place, part] = partial[part, 64:96].astype(BF16)
 
     sends = []
     for n, partner in enumerate(partners):
         sends.append(
             pltpu.make_async_remote_copy(
-                src_ref=higher, dst_ref=group_rows.at[place],
+                src_ref=group_rows.at[place], dst_ref=group_rows.at[place],
                 send_sem=up_send.at[1 + n], recv_sem=up_recv.at[1 + place],
                 device_id=partner, device_id_type=MESH,
             )
         )
     sends.append(
         pltpu.make_async_remote_copy(
-            src_ref=upper, dst_ref=pair_rows.at[odd],
+            src_ref=pair_rows.at[odd], dst_ref=pair_rows.at[odd],
             send_sem=up_send.at[0], recv_sem=up_recv.at[0],
             device_id=sibling, device_id_type=MESH,
         )
     )
     for send in sends:
         send.start()
-    keeps = [
-        pltpu.make_async_copy(upper, pair_rows.at[odd], out_sem.at[5]),
-        pltpu.make_async_copy(higher, group_rows.at[place], out_sem.at[6]),
-    ]
-    for keep in keeps:
-        keep.start()
-
     leaf_stage(s, i, high, low)
     all_high = skel[0].reshape(LEAVES * SKEL, COLS)
     all_low = skel[1].reshape(LEAVES * SKEL, COLS)
     node_high = dot(pick_up[...], all_high).astype(BF16)
     node_low = dot(pick_up[...], all_low).astype(BF16)
-    node_skel[0] = node_high
-    node_skel[1] = node_low
-    keeps.append(pltpu.make_async_copy(node_skel, node_rows, out_sem.at[7]))
-    keeps[-1].start()
+    node_rows[0] = node_high
+    node_rows[1] = node_low
     matrix, scale = normalized(gram(node_high, node_low, node_high, node_low))
-    start[LEAVES] = matrix
     node_coupling[...] = gram(all_high, all_low, node_high, node_low) * scale
-    inverses = invert(start, work, (LEAVES - 1, LEAVES))
-    leaf_out[i] = dot_highest(coupling[s], inverses[0])
-    leaf_put(i).start()
-    node_out[...] = dot_highest(node_coupling[...], inverses[1])
-    keeps.append(pltpu.make_async_copy(node_out, node_result, out_sem.at[4]))
-    keeps[-1].start()
+    inverses = invert([start[LEAVES - 1], matrix])
+    leaf_result[i] = apply(coupling[s], inverses[0])
+    node_result[...] = apply(node_coupling[...], inverses[1])
 
     pltpu.make_async_remote_copy(
-        src_ref=upper, dst_ref=pair_rows.at[even],
+        src_ref=pair_rows.at[even], dst_ref=pair_rows.at[even],
         send_sem=up_send.at[0], recv_sem=up_recv.at[0],
         device_id=sibling, device_id_type=MESH,
     ).wait_recv()
     for n in range(1, 4):
         spot = (place + n) % 4
         pltpu.make_async_remote_copy(
-            src_ref=higher, dst_ref=group_rows.at[spot],
+            src_ref=group_rows.at[spot], dst_ref=group_rows.at[spot],
             send_sem=up_send.at[0], recv_sem=up_recv.at[1 + spot],
             device_id=sibling, device_id_type=MESH,
         ).wait_recv()
@@ -356,55 +351,33 @@
 
     for send in sends:
         send.wait_send()
-    for keep in keeps:
-        keep.wait()
-    for i in range(LEAVES):
-        leaf_put(i).wait()
 
 
 def finish(
     node_rows, pair_rows, group_rows, leaf_result, node_result,
-    leaf_hbm, node_hbm, pairs_hbm, groups_hbm,
-    node_skel, pair_buf, group_buf, leaf_out, node_out, small_coupling, start, work,
-    pairs_out, groups_out, in_sem, out_sem,
+    leaf_hbm, node_hbm, pairs_hbm, groups_hbm, pairs_out, groups_out, out_sem,
 ):
-    gets = [
-        pltpu.make_async_copy(group_rows, group_buf, in_sem.at[0]),
-        pltpu.make_async_copy(pair_rows, pair_buf, in_sem.at[1]),
-        pltpu.make_async_copy(node_rows, node_skel, in_sem.at[2]),
-        pltpu.make_async_copy(leaf_result, leaf_out, in_sem.at[3]),
-        pltpu.make_async_copy(node_result, node_out, in_sem.at[4]),
-    ]
-    for get in gets:
-        get.start()
-    odd = lax.axis_index("tile") % 2
-    gets[0].wait()
-    group_high = jnp.concatenate([group_buf[g, 0] for g in range(4)], axis=0)
-    group_low = jnp.concatenate([group_buf[g, 1] for g in range(4)], axis=0)
-    matrix, scale = normalized(gram(group_high, group_low, group_high, group_low))
-    start[1] = matrix
-    gets[1].wait()
-    pair_high = jnp.concatenate([pair_buf[0, 0], pair_buf[1, 0]], axis=0)
-    pair_low = jnp.concatenate([pair_buf[0, 1], pair_buf[1, 1]], axis=0)
-    small_coupling[128:192] = gram(pair_buf[odd, 0], pair_buf[odd, 1], group_high, group_low) * scale
-    matrix, scale = normalized(gram(pair_high, pair_low, pair_high, pair_low))
-    start[0] = matrix
-    gets[2].wait()
-    small_coupling[0:128] = gram(node_skel[0], node_skel[1], pair_high, pair_low) * scale
-    gets[3].wait()
-    gets[4].wait()
     puts = [
-        pltpu.make_async_copy(leaf_out, leaf_hbm, out_sem.at[0]),
-        pltpu.make_async_copy(node_out, node_hbm, out_sem.at[1]),
+        pltpu.make_async_copy(leaf_result, leaf_hbm, out_sem.at[0]),
+        pltpu.make_async_copy(node_result, node_hbm, out_sem.at[1]),
         pltpu.make_async_copy(pairs_out, pairs_hbm, out_sem.at[2]),
         pltpu.make_async_copy(groups_out, groups_hbm, out_sem.at[3]),
     ]
     puts[0].start()
     puts[1].start()
-    inverses = invert(start, work, (0, 1))
-    pairs_out[...] = dot_highest(small_coupling[0:128], inverses[0])
+    odd = lax.axis_index("tile") % 2
+    group_high = jnp.concatenate([group_rows[g, 0] for g in range(4)], axis=0)
+    group_low = jnp.concatenate([group_rows[g, 1] for g in range(4)], axis=0)
+    pair_high = jnp.concatenate([pair_rows[0, 0], pair_rows[1, 0]], axis=0)
+    pair_low = jnp.concatenate([pair_rows[0, 1], pair_rows[1, 1]], axis=0)
+    group_matrix, scale = normalized(gram(group_high, group_low, group_high, group_low))
+    group_coupling = gram(pair_rows[odd, 0], pair_rows[odd, 1], group_high, group_low) * scale
+    pair_matrix, scale = normalized(gram(pair_high, pair_low, pair_high, pair_low))
+    pair_coupling = gram(node_rows[0], node_rows[1], pair_high, pair_low) * scale
+    inverses = invert([pair_matrix, group_matrix])
+    pairs_out[...] = apply(pair_coupling, inverses[0])
     puts[2].start()
-    groups_out[...] = dot_highest(small_coupling[128:192], inverses[1])
+    groups_out[...] = apply(group_coupling, inverses[1])
     puts[3].start()
     for put in puts:
         put.wait()
@@ -412,6 +385,8 @@
 
 def body(quads, tiles, blocks, offsets, sketch, leaf_pivots, node_pivots, pair_pivots, group_pivots):
     any_space = pl.BlockSpec(memory_space=pl.ANY)
+    vmem = pl.BlockSpec(memory_space=pltpu.VMEM)
+    hbm = pl.BlockSpec(memory_space=pltpu.HBM)
     dma = pltpu.SemaphoreType.DMA
     leaf_shape = ((LEAVES, BLOCK, SKEL), F32)
     node_shape = ((LEAVES * SKEL, SKEL), F32)
@@ -422,8 +397,8 @@
     leaf_result, node_result, node_rows, pair_rows, group_rows = pl.pallas_call(
         functools.partial(kernel, quads, tiles),
         out_shape=[jax.ShapeDtypeStruct(s, d) for s, d in shapes],
-        in_specs=[any_space] * 7,
-        out_specs=[any_space] * 5,
+        in_specs=[hbm] * 7,
+        out_specs=[vmem] * 5,
         scratch_shapes=[
             pltpu.VMEM((LEAVES + 2 * HALF, BLOCK, COLS), BF16),
             pltpu.VMEM((LEAVES, NNZ, BLOCK, BLOCK), BF16),
@@ -440,39 +415,27 @@
             pltpu.VMEM((2, LEAVES, SKEL, COLS), BF16),
             pltpu.VMEM((LEAVES, BLOCK, SKEL), F32),
             pltpu.VMEM((LEAVES * SKEL, SKEL), F32),
-            pltpu.VMEM((LEAVES + 1, SKEL, SKEL), F32),
-            pltpu.VMEM((LEAVES + 1, SKEL, 4 * SKEL), BF16),
-            pltpu.VMEM((2, SKEL // 2, COLS), BF16),
-            pltpu.VMEM((2, SKEL // 4, COLS), BF16),
-            pltpu.VMEM(*rows_shape),
-            pltpu.VMEM(*leaf_shape),
-            pltpu.VMEM(*node_shape),
+            pltpu.VMEM((LEAVES, SKEL, SKEL), F32),
             dma((LEAVES + 1,)), dma((5,)), dma((2 * HALF,)), dma((2 * HALF,)),
-            dma((4,)), dma((5,)), dma((8,)),
+            dma((4,)), dma((5,)),
         ],
-        compiler_params=pltpu.CompilerParams(collective_id=0, has_side_effects=True),
+        compiler_params=pltpu.CompilerParams(collective_id=0, has_side_effects=True, vmem_limit_bytes=20 * 1024 * 1024),
         name="compress",
-    )(offsets, leaf_pivots, node_pivots, pair_pivots, group_pivots,
-      blocks, sketch.reshape(LEAVES, BLOCK, COLS))
+    )(*(pltpu.with_memory_space_constraint(x, pltpu.HBM) for x in (
+        offsets, leaf_pivots, node_pivots, pair_pivots, group_pivots,
+        blocks, sketch.reshape(LEAVES, BLOCK, COLS))))
     outs = [leaf_shape, node_shape, ((SKEL, SKEL), F32), ((SKEL // 2, SKEL), F32)]
     leaf, node, pairs, groups = pl.pallas_call(
         finish,
         out_shape=[jax.ShapeDtypeStruct(s, d) for s, d in outs],
-        in_specs=[any_space] * 5,
-        out_specs=[any_space] * 4,
+        in_specs=[vmem] * 5,
+        out_specs=[hbm] * 4,
         scratch_shapes=[
-            pltpu.VMEM(*rows_shape),
-            pltpu.VMEM(*pair_shape),
-            pltpu.VMEM(*group_shape),
-            pltpu.VMEM(*leaf_shape),
-            pltpu.VMEM(*node_shape),
-            pltpu.VMEM((192, SKEL), F32),
-            pltpu.VMEM((2, SKEL, SKEL), F32),
-            pltpu.VMEM((2, SKEL, 4 * SKEL), BF16),
             pltpu.VMEM((SKEL, SKEL), F32),
             pltpu.VMEM((SKEL // 2, SKEL), F32),
-            dma((5,)), dma((4,)),
+            dma((4,)),
         ],
+        compiler_params=pltpu.CompilerParams(vmem_limit_bytes=10 * 1024 * 1024),
         name="finish",
     )(node_rows, pair_rows, group_rows, leaf_result, node_result)
     return leaf.reshape(LEAVES * BLOCK, SKEL), node, pairs, groups

time: 36.4 us -> 31.9 us (0.88)
  Pallas kernels: 35.6 us -> 31.1 us
    pallas_call x1, Pallas kernels: 30.4 us -> 27.9 us  [body(): pl.pallas_call(functools.partial(kernel, quads, tiles), out_shape=[jax.Sh...]
    pallas_call x1, Pallas kernels: 5.16 us -> 3.19 us  [body(): pl.pallas_call(finish, out_shape=[jax.ShapeDtypeStruct(s, d) for s, d in...]
where the time goes in v3:
time: 31.9 us; the launch traced here: 31.7 us
  Pallas kernels  31.1 us (97%)
  between operations  0.64 us (2%)
    pallas_call x1, Pallas kernels, body(): pl.pallas_call(functools.partial(kernel, quads, tiles), out_shape=[jax.Sh...  27.9 us
    pallas_call x1, Pallas kernels, body(): pl.pallas_call(finish, out_shape=[jax.ShapeDtypeStruct(s, d) for s, d in...  3.19 us

profile of v3, /device:TPU:24, one launch (start us, length us, event | category | flops | bytes accessed | tf_op | source)
XLA Modules:
  0.0 31.7 jit_solution(13383435649385885666)
XLA Ops:
  0.6 27.9 %compress.1 = (f32[4,256,128]{2,1,0:T(8,128)S(1)}, f32[512,128]{1,0:T(8,128)S(1)}, bf16[2,128,512]{2,1,0:T(8,128)(2,1)S(1)}, bf16[2,2,64,512]{3,2,1,0:T(8,128)(2,1)S(1)}, bf16[4,2,32,512]{3,2,1,0:T(8,128)(2,1)S(1)}) custom-call(s32[4,6]{1,0:T(4,128)} %offsets_hbm.1, s32[4,128]{1,0:T(4,128)} %leaf_hbm.1, s32[1,128]{1,0:T(1,128)} %node_hbm.1, ...), custom_call_target="tpu_custom_call" | custom-call | tf_op jit(solution)/shard_map/compress/pallas_call | solution.py:397
  28.6 3.2 %finish.1 = (f32[4,256,128]{2,1,0:T(8,128)}, f32[512,128]{1,0:T(8,128)}, f32[128,128]{1,0:T(8,128)}, f32[64,128]{1,0:T(8,128)}) custom-call(bf16[2,128,512]{2,1,0:T(8,128)(2,1)S(1)} %get-tuple-element.13.node_rows, bf16[2,2,64,512]{3,2,1,0:T(8,128)(2,1)S(1)} %get-tuple-element.14.pair_rows, bf16[4,2,32,512]{3,2,1,0:T(8,128)(2,1)S(1)} %get-tuple-element.15.group_rows, ...), custom_call_target="tpu_custom_call" | custom-call | tf_op jit(solution)/shard_map/finish/pallas_call | solution.py:428

commit v4 on v3

--- a/solution.py
+++ b/solution.py
@@ -72,53 +72,87 @@
     return jnp.concatenate(parts, axis=0)
 
 
-def invert(matrices):
+def pair_product(left_high, left_low, right_high, right_low):
+    empty = jnp.zeros_like(right_low)
+    both = dot(
+        across([left_high, left_low]),
+        down([across([right_high, right_low]), across([right_high, empty])]),
+    )
+    return both[:, :SKEL] + both[:, SKEL:]
+
+
+def invert(matrices, fillers=()):
     unit = jnp.where(eye(), 1.0, 0.0)
     rho = 128.0 / 130.0
     ts = list(matrices)
     xs = [None] * len(ts)
+    waiting = list(fillers)
     for step in range(STEPS):
         gain = 2.0 / (2.0 - rho * rho)
         rho = gain - 1.0
-        for j, t in enumerate(ts):
+        products = []
+        for t, x in zip(ts, xs):
             th, tl = split(t)
-            left = across([th, tl, th])
             if step == 0:
-                square = dot(left, down([th, th, tl]))
-                xs[j] = gain * (2.0 * unit - t)
-                ts[j] = gain * (2.0 * t - square)
+                products.append((pair_product(th, tl, th, tl), None))
                 continue
-            xh, xl = split(xs[j])
+            xh, xl = split(x)
             if step == STEPS - 1:
-                product = dot(left, down([xh, xh, xl]))
+                products.append((None, pair_product(th, tl, xh, xl)))
+                continue
+            high = across([th, xh])
+            both = dot(across([th, tl, th]), down([high, high, across([tl, xl])]))
+            products.append((both[:, :SKEL], both[:, SKEL:]))
+        if waiting:
+            waiting.pop(0)()
+        for j, (square, product) in enumerate(products):
+            if step == 0:
+                xs[j] = (2.0 * gain) * unit - gain * ts[j]
             else:
-                both = dot(left, down([across([th, xh]), across([th, xh]), across([tl, xl])]))
-                ts[j] = gain * (2.0 * t - both[:, :SKEL])
-                product = both[:, SKEL:]
-            xs[j] = gain * (2.0 * xs[j] - product)
-    inverses = []
+                xs[j] = (2.0 * gain) * xs[j] - gain * product
+            if square is not None:
+                ts[j] = (2.0 * gain) * ts[j] - gain * square
+    pieces = []
     for x, matrix in zip(xs, matrices):
         xh, xl = split(x)
         high, middle, low = split3(matrix)
-        near = dot(across([high, middle, high, middle, low]), down([xh, xh, xl, xl, xh]))
-        eh, el = split(unit - near)
-        fix = dot(across([xh, xl, xh]), down([eh, eh, el]))
-        inverses.append((xh.astype(F32) + xl.astype(F32)) + fix)
-    return inverses
+        parts = across([xh, xl])
+        near = dot(across([high, middle]), down([parts, parts]))
+        pieces.append((xh, xl, (near[:, :SKEL] + near[:, SKEL:]) + dot(low, xh)))
+    for filler in waiting:
+        filler()
+    return [(xh, xl, unit - near) for xh, xl, near in pieces]
+
+
+def corrected(near_inverse):
+    xh, xl, rest = near_inverse
+    eh, el = split(rest)
+    return (xh.astype(F32) + xl.astype(F32)) + pair_product(xh, xl, eh, el)
+
+
+def apply_near(rows, near_inverse):
+    xh, xl, rest = near_inverse
+    rh, rm, rl = split3(rows)
+    parts = across([xh, xl])
+    main = dot(across([rh, rm]), down([parts, parts]))
+    product = (main[:, :SKEL] + main[:, SKEL:]) + dot(rl, xh)
+    return product + pair_product(*split(product), *split(rest))
 
 
 def apply(rows, inverse):
     rh, rm, rl = split3(rows)
     xh, xm, xl = split3(inverse)
-    return dot(across([rh, rh, rh, rm, rm, rl]), down([xh, xm, xl, xh, xm, xh]))
+    parts = across([xh, xm])
+    main = dot(across([rh, rm]), down([parts, parts]))
+    return (main[:, :SKEL] + main[:, SKEL:]) + dot(across([rh, rl]), down([xl, xh]))
 
 
 def kernel(
     quads, tiles,
     offsets_hbm, leaf_hbm, node_hbm, pair_hbm, group_hbm, blocks_hbm, sketch_hbm,
-    leaf_result, node_result, node_rows, pair_rows, group_rows,
-    window, mats, offsets, leaf_index, node_index, pair_index, group_index, pivots, pick_leaf, pick_up, pick_send, partial,
-    skel, coupling, node_coupling, start,
+    leaf_result, last_coupling, node_coupling, near, node_rows, pair_rows, group_rows,
+    window, mats, offsets, leaf_index, node_index, pair_index, group_index, pivots, pick_leaf, pick_node, pick_send, partial, node_partial,
+    skel, coupling, start,
     local_sem, index_sem, send_sem, recv_sem, up_send, up_recv,
 ):
     q = lax.axis_index("quad")
@@ -159,17 +193,11 @@
     ]
     for small in smalls:
         small.start()
-    own = pltpu.make_async_copy(sketch_hbm, window.at[pl.ds(HALF, LEAVES)], local_sem.at[LEAVES])
-    own.start()
-
     def leaf_at(s):
         return even * (LEAVES - 1 - s) + odd * s
 
     def load(i):
         return pltpu.make_async_copy(blocks_hbm.at[i], mats.at[i], local_sem.at[i])
-
-    for s in range(LEAVES):
-        load(leaf_at(s)).start()
 
     ends = jnp.where(me > 0, 1, 0) + jnp.where(me < last, 1, 0)
     pl.semaphore_wait(barrier, 3 + ends)
@@ -197,6 +225,12 @@
     def _():
         for j in range(HALF):
             to_left(j).start()
+
+    own = pltpu.make_async_copy(sketch_hbm, window.at[pl.ds(HALF, LEAVES)], local_sem.at[LEAVES])
+    own.start()
+
+    for s in range(LEAVES):
+        load(leaf_at(s)).start()
 
     @pl.when(me == 0)
     def _():
@@ -225,11 +259,12 @@
     node_pick = one_hot(4, LEAVES * SKEL)
     upper_pick = dot(one_hot(5, SKEL)[0:64], node_pick).astype(BF16)
     higher_pick = dot(one_hot(6, 128)[0:32, 0:64], upper_pick).astype(BF16)
-    pick_up[...] = node_pick
     both_pick = jnp.concatenate([upper_pick, higher_pick], axis=0)
     for i in range(LEAVES):
         pick_send[i] = dot(both_pick[:, i * SKEL:(i + 1) * SKEL], pick_leaf[i]).astype(BF16)
+        pick_node[i] = dot(node_pick[:, i * SKEL:(i + 1) * SKEL], pick_leaf[i]).astype(BF16)
     partial[...] = jnp.zeros_like(partial)
+    node_partial[...] = jnp.zeros_like(node_partial)
 
     own.wait()
 
@@ -275,17 +310,28 @@
         skel[1, i] = skel_low
         matrix, scale = normalized(gram(skel_high, skel_low, skel_high, skel_low))
         start[s] = matrix
-        coupling[s] = gram(high, low, skel_high, skel_low) * scale
+
+        def couple(first, count):
+            part = gram(high[first:first + count], low[first:first + count], skel_high, skel_low)
+            if s < LEAVES - 1:
+                coupling[s, first:first + count] = part * scale
+            else:
+                last_coupling[first:first + count] = part * scale
+
+        return [functools.partial(couple, first, 128) for first in (0, 128)]
 
     for s in range(LEAVES - 1):
         i = leaf_at(s)
         high, low = last_term(s, i, first_terms(i))
-        leaf_stage(s, i, high, low)
+        node_partial[0] += dot(pick_node[i], high)
+        node_partial[1] += dot(pick_node[i], low)
+        for fill in leaf_stage(s, i, high, low):
+            fill()
 
     inverses = invert([start[s] for s in range(LEAVES - 1)])
     for s in range(LEAVES - 1):
         i = leaf_at(s)
-        leaf_result[i] = apply(coupling[s], inverses[s])
+        leaf_result[i] = apply(coupling[s], corrected(inverses[s]))
 
     s = LEAVES - 1
     i = leaf_at(s)
@@ -313,18 +359,22 @@
     )
     for send in sends:
         send.start()
-    leaf_stage(s, i, high, low)
-    all_high = skel[0].reshape(LEAVES * SKEL, COLS)
-    all_low = skel[1].reshape(LEAVES * SKEL, COLS)
-    node_high = dot(pick_up[...], all_high).astype(BF16)
-    node_low = dot(pick_up[...], all_low).astype(BF16)
+    fillers = leaf_stage(s, i, high, low)
+    node_high = (node_partial[0] + dot(pick_node[i], high)).astype(BF16)
+    node_low = (node_partial[1] + dot(pick_node[i], low)).astype(BF16)
     node_rows[0] = node_high
     node_rows[1] = node_low
-    matrix, scale = normalized(gram(node_high, node_low, node_high, node_low))
-    node_coupling[...] = gram(all_high, all_low, node_high, node_low) * scale
-    inverses = invert([start[LEAVES - 1], matrix])
-    leaf_result[i] = apply(coupling[s], inverses[0])
-    node_result[...] = apply(node_coupling[...], inverses[1])
+    matrix, node_scale = normalized(gram(node_high, node_low, node_high, node_low))
+
+    def couple_node(leaf):
+        part = gram(skel[0, leaf], skel[1, leaf], node_high, node_low)
+        node_coupling[leaf * SKEL:(leaf + 1) * SKEL] = part * node_scale
+
+    fillers += [functools.partial(couple_node, leaf) for leaf in range(LEAVES)]
+    inverses = invert([start[LEAVES - 1], matrix], fillers)
+    for n, (xh, xl, rest) in enumerate(inverses):
+        near[n, 0] = xh.astype(F32) + xl.astype(F32)
+        near[n, 1] = rest
 
     pltpu.make_async_remote_copy(
         src_ref=pair_rows.at[even], dst_ref=pair_rows.at[even],
@@ -354,31 +404,61 @@
 
 
 def finish(
-    node_rows, pair_rows, group_rows, leaf_result, node_result,
-    leaf_hbm, node_hbm, pairs_hbm, groups_hbm, pairs_out, groups_out, out_sem,
+    leaf_result, last_coupling, node_coupling, near, node_rows, pair_rows, group_rows,
+    leaf_hbm, node_hbm, pairs_hbm, groups_hbm, last_out, node_out, pairs_out, groups_out, out_sem,
 ):
-    puts = [
-        pltpu.make_async_copy(leaf_result, leaf_hbm, out_sem.at[0]),
-        pltpu.make_async_copy(node_result, node_hbm, out_sem.at[1]),
-        pltpu.make_async_copy(pairs_out, pairs_hbm, out_sem.at[2]),
-        pltpu.make_async_copy(groups_out, groups_hbm, out_sem.at[3]),
-    ]
-    puts[0].start()
-    puts[1].start()
     odd = lax.axis_index("tile") % 2
+    first = 1 - odd
+    last_leaf = odd * (LEAVES - 1)
+    early = pltpu.make_async_copy(
+        leaf_result.at[pl.ds(first, LEAVES - 1)], leaf_hbm.at[pl.ds(first, LEAVES - 1)], out_sem.at[0]
+    )
+    early.start()
+    half = LEAVES * SKEL // 2
+    puts = [pltpu.make_async_copy(last_out, leaf_hbm.at[last_leaf], out_sem.at[1])]
+    for n in range(2):
+        rows = pl.ds(half * n, half)
+        puts.append(pltpu.make_async_copy(node_out.at[rows], node_hbm.at[rows], out_sem.at[2 + n]))
+    puts.append(pltpu.make_async_copy(pairs_out, pairs_hbm, out_sem.at[4]))
+    puts.append(pltpu.make_async_copy(groups_out, groups_hbm, out_sem.at[5]))
     group_high = jnp.concatenate([group_rows[g, 0] for g in range(4)], axis=0)
     group_low = jnp.concatenate([group_rows[g, 1] for g in range(4)], axis=0)
     pair_high = jnp.concatenate([pair_rows[0, 0], pair_rows[1, 0]], axis=0)
     pair_low = jnp.concatenate([pair_rows[0, 1], pair_rows[1, 1]], axis=0)
-    group_matrix, scale = normalized(gram(group_high, group_low, group_high, group_low))
-    group_coupling = gram(pair_rows[odd, 0], pair_rows[odd, 1], group_high, group_low) * scale
-    pair_matrix, scale = normalized(gram(pair_high, pair_low, pair_high, pair_low))
-    pair_coupling = gram(node_rows[0], node_rows[1], pair_high, pair_low) * scale
-    inverses = invert([pair_matrix, group_matrix])
-    pairs_out[...] = apply(pair_coupling, inverses[0])
-    puts[2].start()
-    groups_out[...] = apply(group_coupling, inverses[1])
+    group_matrix, group_scale = normalized(gram(group_high, group_low, group_high, group_low))
+    pair_matrix, pair_scale = normalized(gram(pair_high, pair_low, pair_high, pair_low))
+    coupled = []
+    fixed = []
+
+    def fix():
+        for n in range(2):
+            fixed.append(corrected((*split(near[n, 0]), near[n, 1])))
+
+    def last_rows():
+        last_out[...] = apply(last_coupling[...], fixed[0])
+        puts[0].start()
+
+    def node_part(n):
+        rows = slice(half * n, half * n + half)
+        node_out[rows] = apply(node_coupling[rows], fixed[1])
+        puts[1 + n].start()
+
+    inverses = invert([pair_matrix, group_matrix], [
+        fix,
+        functools.partial(node_part, 0),
+        functools.partial(node_part, 1),
+        last_rows,
+        lambda: coupled.append(gram(node_rows[0], node_rows[1], pair_high, pair_low) * pair_scale),
+        lambda: coupled.append(
+            gram(pair_rows[odd, 0], pair_rows[odd, 1], group_high, group_low) * group_scale
+        ),
+    ])
+    pair_coupling, group_coupling = coupled
+    pairs_out[...] = apply_near(pair_coupling, inverses[0])
     puts[3].start()
+    groups_out[...] = apply_near(group_coupling, inverses[1])
+    puts[4].start()
+    early.wait()
     for put in puts:
         put.wait()
 
@@ -393,12 +473,14 @@
     rows_shape = ((2, SKEL, COLS), BF16)
     pair_shape = ((2, 2, SKEL // 2, COLS), BF16)
     group_shape = ((4, 2, SKEL // 4, COLS), BF16)
-    shapes = [leaf_shape, node_shape, rows_shape, pair_shape, group_shape]
-    leaf_result, node_result, node_rows, pair_rows, group_rows = pl.pallas_call(
+    block_shape = ((BLOCK, SKEL), F32)
+    near_shape = ((2, 2, SKEL, SKEL), F32)
+    shapes = [leaf_shape, block_shape, node_shape, near_shape, rows_shape, pair_shape, group_shape]
+    results = pl.pallas_call(
         functools.partial(kernel, quads, tiles),
         out_shape=[jax.ShapeDtypeStruct(s, d) for s, d in shapes],
         in_specs=[hbm] * 7,
-        out_specs=[vmem] * 5,
+        out_specs=[vmem] * 7,
         scratch_shapes=[
             pltpu.VMEM((LEAVES + 2 * HALF, BLOCK, COLS), BF16),
             pltpu.VMEM((LEAVES, NNZ, BLOCK, BLOCK), BF16),
@@ -409,12 +491,12 @@
             pltpu.VMEM((1, 32), jnp.int32),
             pltpu.VMEM((8, 128), F32),
             pltpu.VMEM((LEAVES, SKEL, BLOCK), BF16),
-            pltpu.VMEM((SKEL, LEAVES * SKEL), BF16),
+            pltpu.VMEM((LEAVES, SKEL, BLOCK), BF16),
             pltpu.VMEM((LEAVES, 96, BLOCK), BF16),
             pltpu.VMEM((2, 96, COLS), F32),
+            pltpu.VMEM((2, SKEL, COLS), F32),
             pltpu.VMEM((2, LEAVES, SKEL, COLS), BF16),
-            pltpu.VMEM((LEAVES, BLOCK, SKEL), F32),
-            pltpu.VMEM((LEAVES * SKEL, SKEL), F32),
+            pltpu.VMEM((LEAVES - 1, BLOCK, SKEL), F32),
             pltpu.VMEM((LEAVES, SKEL, SKEL), F32),
             dma((LEAVES + 1,)), dma((5,)), dma((2 * HALF,)), dma((2 * HALF,)),
             dma((4,)), dma((5,)),
@@ -428,16 +510,18 @@
     leaf, node, pairs, groups = pl.pallas_call(
         finish,
         out_shape=[jax.ShapeDtypeStruct(s, d) for s, d in outs],
-        in_specs=[vmem] * 5,
+        in_specs=[vmem] * 7,
         out_specs=[hbm] * 4,
         scratch_shapes=[
+            pltpu.VMEM(*block_shape),
+            pltpu.VMEM(*node_shape),
             pltpu.VMEM((SKEL, SKEL), F32),
             pltpu.VMEM((SKEL // 2, SKEL), F32),
-            dma((4,)),
+            dma((6,)),
         ],
         compiler_params=pltpu.CompilerParams(vmem_limit_bytes=10 * 1024 * 1024),
         name="finish",
-    )(node_rows, pair_rows, group_rows, leaf_result, node_result)
+    )(*results)
     return leaf.reshape(LEAVES * BLOCK, SKEL), node, pairs, groups
 
 

time: 31.9 us -> 31.6 us (level)
  the two profiles are of different devices: /device:TPU:24 before, /device:TPU:57 now
where the time goes in v4:
time: 31.6 us; the launch traced here: 31.5 us
  Pallas kernels  30.8 us (97%)
  between operations  0.64 us (2%)
    pallas_call x1, Pallas kernels, body(): pl.pallas_call(functools.partial(kernel, quads, tiles), out_shape=[jax.Sh...  27.9 us
    pallas_call x1, Pallas kernels, body(): pl.pallas_call(finish, out_shape=[jax.ShapeDtypeStruct(s, d) for s, d in...  2.9 us

profile of v4, /device:TPU:57, one launch (start us, length us, event | category | flops | bytes accessed | tf_op | source)
XLA Modules:
  0.0 31.5 jit_solution(18244622887868291046)
XLA Ops:
  0.6 27.9 %compress.1 = (f32[4,256,128]{2,1,0:T(8,128)S(1)}, f32[256,128]{1,0:T(8,128)S(1)}, f32[512,128]{1,0:T(8,128)S(1)}, f32[2,2,128,128]{3,2,1,0:T(8,128)S(1)}, bf16[...) custom-call(s32[4,6]{1,0:T(4,128)} %offsets_hbm.1, ...), custom_call_target="tpu_custom_call" | custom-call | tf_op jit(solution)/shard_map/compress/pallas_call | solution.py:479
  28.6 2.9 %finish.1 = (f32[4,256,128]{2,1,0:T(8,128)}, f32[512,128]{1,0:T(8,128)}, f32[128,128]{1,0:T(8,128)}, f32[64,128]{1,0:T(8,128)}) custom-call(f32[4,256,128]{2,1,0:T(8,128)S(1)} %get-tuple-element.15.leaf_result, f32[256,128]{1,0:T(8,128)S(1)} %get-tuple-element.16.last_coupling, f32[512,128]{1,0:T(8,128)S(1)} %get-tuple-element.17.node_coupling, ...), custom_call_target="tpu_custom_call" | custom-call | tf_op jit(solution)/shard_map/finish/pallas_call | solution.py:510

commit v5 on v4

--- a/solution.py
+++ b/solution.py
@@ -291,16 +291,12 @@
             total = total + term(i, j)
         return total
 
-    def last_term(s, i, total):
+    def panel_arrives(s):
         if s > 0:
             @pl.when((me > 0) & (me < last))
             def _():
                 arrived(even * (HALF - s) + odd * (HALF + LEAVES - 1 + s),
                         even * (HALF - s) + odd * (HALF - 1 + s)).wait_recv()
-        high, low = split(total + term(i, NNZ - 1))
-        partial[0] += dot(pick_send[i], high)
-        partial[1] += dot(pick_send[i], low)
-        return high, low
 
     def leaf_stage(s, i, high, low):
         pick = pick_leaf[i]
@@ -322,7 +318,10 @@
 
     for s in range(LEAVES - 1):
         i = leaf_at(s)
-        high, low = last_term(s, i, first_terms(i))
+        total = first_terms(i)
+        panel_arrives(s)
+        high, low = split(total + term(i, NNZ - 1))
+        partial[...] += dot(pick_send[i], high) + dot(pick_send[i], low)
         node_partial[0] += dot(pick_node[i], high)
         node_partial[1] += dot(pick_node[i], low)
         for fill in leaf_stage(s, i, high, low):
@@ -335,11 +334,19 @@
 
     s = LEAVES - 1
     i = leaf_at(s)
-    high, low = last_term(s, i, first_terms(i))
+    total = first_terms(i)
+    block = odd * (NNZ - 1)
+    picked = dot(pick_send[i], mats[i, block]).astype(BF16)
+    high, low = split(total)
+    rows = partial[...] + (dot(pick_send[i], high) + dot(pick_send[i], low))
+    partial[...] = rows
+    panel_arrives(s)
+    near_panel = offsets[i, block] == block - HALF
+    panel = jnp.where(near_panel, window[i + block], window[i + block + 1])
     place = t % 4
-    for part in range(2):
-        pair_rows[odd, part] = partial[part, 0:64].astype(BF16)
-        group_rows[place, part] = partial[part, 64:96].astype(BF16)
+    for part, value in enumerate(split(partial[...] + dot(picked, panel))):
+        pair_rows[odd, part] = value[0:64]
+        group_rows[place, part] = value[64:96]
 
     sends = []
     for n, partner in enumerate(partners):
@@ -359,6 +366,7 @@
     )
     for send in sends:
         send.start()
+    high, low = split(total + dot(mats[i, block], panel))
     fillers = leaf_stage(s, i, high, low)
     node_high = (node_partial[0] + dot(pick_node[i], high)).astype(BF16)
     node_low = (node_partial[1] + dot(pick_node[i], low)).astype(BF16)
@@ -493,7 +501,7 @@
             pltpu.VMEM((LEAVES, SKEL, BLOCK), BF16),
             pltpu.VMEM((LEAVES, SKEL, BLOCK), BF16),
             pltpu.VMEM((LEAVES, 96, BLOCK), BF16),
-            pltpu.VMEM((2, 96, COLS), F32),
+            pltpu.VMEM((96, COLS), F32),
             pltpu.VMEM((2, SKEL, COLS), F32),
             pltpu.VMEM((2, LEAVES, SKEL, COLS), BF16),
             pltpu.VMEM((LEAVES - 1, BLOCK, SKEL), F32),

time: 31.6 us -> 31.6 us (level)
  no operation moved by 1% of the time
where the time goes in v5:
time: 31.6 us; the launch traced here: 31.5 us
  Pallas kernels  30.8 us (97%)
  between operations  0.64 us (2%)
    pallas_call x1, Pallas kernels, body(): pl.pallas_call(functools.partial(kernel, quads, tiles), out_shape=[jax.Sh...  27.9 us
    pallas_call x1, Pallas kernels, body(): pl.pallas_call(finish, out_shape=[jax.ShapeDtypeStruct(s, d) for s, d in...  2.9 us

profile of v5, /device:TPU:57, one launch (start us, length us, event | category | flops | bytes accessed | tf_op | source)
XLA Modules:
  0.0 31.5 jit_solution(15546501541020610048)
XLA Ops:
  0.6 27.9 %compress.1 = (f32[4,256,128]{2,1,0:T(8,128)S(1)}, f32[256,128]{1,0:T(8,128)S(1)}, f32[512,128]{1,0:T(8,128)S(1)}, f32[2,2,128,128]{3,2,1,0:T(8,128)S(1)}, bf16[...) custom-call(s32[4,6]{1,0:T(4,128)} %offsets_hbm.1, ...), custom_call_target="tpu_custom_call" | custom-call | tf_op jit(solution)/shard_map/compress/pallas_call | solution.py:487
  28.6 2.9 %finish.1 = (f32[4,256,128]{2,1,0:T(8,128)}, f32[512,128]{1,0:T(8,128)}, f32[128,128]{1,0:T(8,128)}, f32[64,128]{1,0:T(8,128)}) custom-call(f32[4,256,128]{2,1,0:T(8,128)S(1)} %get-tuple-element.15.leaf_result, f32[256,128]{1,0:T(8,128)S(1)} %get-tuple-element.16.last_coupling, f32[512,128]{1,0:T(8,128)S(1)} %get-tuple-element.17.node_coupling, ...), custom_call_target="tpu_custom_call" | custom-call | tf_op jit(solution)/shard_map/finish/pallas_call | solution.py:518
